TPU v7x, 32 devices: a whole 2x2x4 slice. The times are simulated.
32 devices in a mesh: parts: 2 (over x), chol: 16 (over z, y, core).
Axes of the slice: x: 2, y: 2, z: 4, core: 2. Of those that a mesh axis runs over, the one named last changes fastest.
Arguments:
- orbitals: float32 [32, 100, 1024], P(('parts', 'chol')), parts along dimension 0, may hold values from -6 to 6
- intersection_inv: float32 [32, 100, 100], P(('parts', 'chol')), parts along dimension 0, may hold values from -0.625 to 0.625
- factor_rows: bfloat16 [4096, 1024], P('chol'), may hold values from -0.1875 to 0.1875
- factor_rotated: bfloat16 [100, 4096], replicated, may hold values from -0.625 to 0.625
- factor_core: bfloat16 [1024, 4096], P('chol'), may hold values from -0.125 to 0.125
- fields: float32 [32, 1024], P('parts', 'chol'), parts along dimension 0, may hold values from -6 to 6
Outputs:
- propagated: float32 [32, 100, 1024], P(('parts', 'chol')), parts along dimension 0
- force_bias: float32 [32, 1024], P('parts', 'chol'), parts along dimension 0
There are 2 independent parts, one for each index of `parts`. A program takes and returns all parts, laid end to end along the dimension named above; an argument that names none is the same for every part. Nothing has to cross between parts.
All inputs are finite; a program needn't handle non-finite values.
Results may differ from a plain program's by a relative error of at most 0.0091.
Values may be sent and summed in bfloat16 or wider, within the bound.
A program may use at most 64 MiB of HBM per device.

v0:
```python
import functools

import jax
import jax.numpy as jnp
from jax import lax
from jax.experimental import pallas as pl
from jax.experimental.pallas import tpu as pltpu
from jax.sharding import PartitionSpec as P

TAYLOR = 4
F32, BF16 = jnp.float32, jnp.bfloat16
LAST = (((1,), (1,)), ((), ()))


def kernel(
    n, orb_ref, inv_ref, rows_ref, rot_ref, core_ref, fields_ref, out_ref, fb_ref,
    xbuf, orb3, lhs, pad, rot, corep, s1, sc, dbuf, dfull, pbuf, rbuf, pot, tpart, tsend, trecv, tbf, total,
    orb_sem, own_sem, rot_sem, core_sem, ring_send, ring_recv, twin_send, twin_recv, pair_send, pair_recv,
    dens_send, dens_recv, ready_sem, pot_send, pot_recv, term_send, term_recv,
):
    h = n // 2
    p, m = rows_ref.shape
    ne = orb_ref.shape[0]
    nep = pad.shape[0]
    half = h * p
    side_rows = p * 5 // 256 * 16
    sizes = (side_rows, p - 2 * side_rows)
    here = lax.axis_index("parts")
    starts = (here * side_rows, 2 * side_rows)
    me = lax.axis_index("chol")
    q, c = me // 2, me % 2
    partner = q * 2 + (1 - c)
    r = (1 - q % 2) * (q // 2) + (q % 2) * (h - 1 - q // 2)

    def chip_at(pos):
        pos = (pos + 2 * h) % h
        s = pos // (h // 2)
        return (1 - s) * 2 * pos + s * (2 * (h - 1 - pos) + 1)

    barrier = pltpu.get_barrier_semaphore()
    for near in (partner, chip_at(r + 1) * 2 + c, chip_at(r - 1) * 2 + c):
        pl.semaphore_signal(barrier, inc=1, device_id={"chol": near}, device_id_type=pl.DeviceIdType.MESH)
    pl.semaphore_signal(barrier, inc=1, device_id={"parts": 1 - here}, device_id_type=pl.DeviceIdType.MESH)

    orb_copy = pltpu.make_async_copy(orb_ref, orb3, orb_sem)
    orb_copy.start()
    own_copy = pltpu.make_async_copy(rows_ref, xbuf.at[pl.ds(pl.multiple_of(q * p, p), p)], own_sem)
    own_copy.start()
    rot_copy = pltpu.make_async_copy(rot_ref, rot, rot_sem)
    rot_copy.start()
    core_copies = []
    for s in range(n):
        copy = pltpu.make_async_copy(
            core_ref.at[:, pl.ds(s * p, p)],
            corep.at[:, pl.ds((s % 2) * half + (s // 2) * p, p)],
            core_sem.at[s],
        )
        copy.start()
        core_copies.append(copy)

    pl.semaphore_wait(barrier, 4)

    def remote(src, dst, send, recv, target):
        return pltpu.make_async_remote_copy(
            src_ref=src, dst_ref=dst, send_sem=send, recv_sem=recv,
            device_id={"chol": target}, device_id_type=pl.DeviceIdType.MESH,
        )

    def rows(way, step, part):
        if step < h // 2:
            return pl.multiple_of(starts[part], 16), sizes[part]
        if part == 1:
            return 2 * side_rows + way * (sizes[1] // 2), sizes[1] // 2
        return pl.multiple_of((way + (1 - 2 * way) * here) * side_rows, 16), side_rows

    def slot(chip, way, step, part):
        first, size = rows(way, step, part)
        return xbuf.at[pl.ds(pl.multiple_of(chip * p + first, 16), size)]

    def twin(way, step, row):
        view = xbuf.at[pl.ds(pl.multiple_of(chip_at(r - (1 - 2 * way) * step) * p + row, 16), side_rows)]
        return pltpu.make_async_remote_copy(
            src_ref=view, dst_ref=view, send_sem=twin_send.at[way, step - 1], recv_sem=twin_recv.at[way, step - 1],
            device_id={"parts": 1 - here}, device_id_type=pl.DeviceIdType.MESH,
        )

    def hop(way, step, part):
        sign = 1 - 2 * way
        origin = chip_at(r - sign * (step - 1))
        src = rows_ref.at[pl.ds(*rows(way, step, part))] if step == 1 else slot(origin, way, step, part)
        return remote(
            src, slot(origin, way, step, part), ring_send.at[way, step - 1, part], ring_recv.at[way, step - 1, part],
            chip_at(r + sign) * 2 + c,
        )

    def arrival(way, step, part):
        sign = 1 - 2 * way
        landed = slot(chip_at(r - sign * step), way, step, part)
        return remote(
            landed, landed, ring_send.at[way, step - 1, part], ring_recv.at[way, step - 1, part],
            chip_at(r + sign) * 2 + c,
        )

    sent = []
    for part in range(2):
        for way in range(2):
            copy = hop(way, 1, part)
            copy.start()
            sent.append(copy)

    pad[...] = jnp.zeros_like(pad)
    orb_copy.wait()
    for j in range(m // 128):
        pad[0:ne, j * 128 : (j + 1) * 128] = orb3[:, j]
    total[...] = pad[...]
    lhs[c, nep : 2 * nep] = pad[...].astype(BF16)
    pad[0:ne] = jnp.dot(inv_ref[0], pad[0:ne], preferred_element_type=F32, precision=lax.Precision.HIGHEST)
    lhs[c, 0:nep] = pad[...].astype(BF16)
    pair = remote(lhs.at[c], lhs.at[c], pair_send, pair_recv, partner)
    pair.start()
    sent.append(pair)
    own_copy.wait()
    rot_copy.wait()
    remote(lhs.at[1 - c], lhs.at[1 - c], pair_send, pair_recv, partner).wait_recv()

    def block(chip, place):
        where = pl.ds(pl.multiple_of(chip * p, p), p)
        result = lax.dot_general(
            lhs[...].reshape(4 * nep, m), xbuf[where, :], LAST, preferred_element_type=F32
        )
        rotated = rot[:, pl.ds(pl.multiple_of((chip * 2 + c) * p, p), p)].astype(F32)
        for w in range(2):
            projected = result[w * 2 * nep : w * 2 * nep + ne]
            density = jnp.sum(rotated * projected, axis=0, keepdims=True)
            dbuf[me, w : w + 1, place * p : (place + 1) * p] = density.astype(BF16).astype(F32)
            s1[w * nep : (w + 1) * nep, where] = result[w * 2 * nep + nep : (w + 1) * 2 * nep]

    def finish(step):
        if step < h // 2:
            for way in range(2 if step < h // 2 - 1 else 1):
                twin(way, step, (1 - here) * side_rows).wait_recv()
            block(chip_at(r - step), 2 * step - 1)
            block(chip_at(r + step), 2 * step)
        else:
            block(chip_at(r - step), h - 1)

    cut = (h - 1) * p
    spans = (pl.ds(0, cut), pl.ds(cut, p))

    def spread(group):
        for k in range(1, n):
            view = dbuf.at[me, :, spans[group]]
            copy = remote(view, view, dens_send.at[group, k - 1], dens_recv.at[group, k - 1], (me + k) % n)
            copy.start()
            sent.append(copy)

    block(q, 0)
    for step in range(1, h // 2 + 1):
        for part in range(2):
            for way in (1, 0):
                arrival(way, step, part).wait_recv()
                if step < h // 2 - 1 or (step == h // 2 - 1 and (way, part) != (1, 0)):
                    copy = hop(way, step + 1, part)
                    copy.start()
                    sent.append(copy)
                if part == 0 and step < h // 2:
                    copy = twin(way, step, here * side_rows)
                    copy.start()
                    sent.append(copy)
        if step == h // 2:
            pl.semaphore_signal(ready_sem, inc=1, device_id={"chol": partner}, device_id_type=pl.DeviceIdType.MESH)
        if step > 1:
            finish(step - 1)
        if step == h // 2 - 1:
            twin(1, step, (1 - here) * side_rows).wait_recv()
            copy = hop(1, step + 1, 0)
            copy.start()
            sent.append(copy)
    pl.semaphore_wait(ready_sem, 1)
    spread(0)
    finish(h // 2)
    spread(1)
    for copy in core_copies:
        copy.wait()
    for group in range(2):
        for k in range(1, n):
            source = (me + n - k) % n
            view = dbuf.at[source, :, spans[group]]
            remote(view, view, dens_send.at[group, k - 1], dens_recv.at[group, k - 1], source).wait_recv()
    for s in range(n):
        chip, side = s // 2, s % 2
        pos = chip // 2 if chip % 2 == 0 else h - 1 - chip // 2
        for place in range(h):
            step = (place + 1) // 2
            other = chip_at(pos - step if place % 2 else pos + step)
            first = side * half + other * p
            dfull[2 * chip : 2 * chip + 2, first : first + p] = dbuf[s, :, place * p : (place + 1) * p]
    force_bias = lax.dot_general(dfull[...].astype(BF16), corep[...], LAST, preferred_element_type=F32)
    fb_ref[...] = force_bias
    shifted = (fields_ref[...] - force_bias).astype(BF16)
    for side in range(2):
        dfull[:, side * half : (side + 1) * half] = jnp.dot(
            shifted, corep[:, side * half : (side + 1) * half], preferred_element_type=F32
        )
    for s in range(n):
        pbuf[s] = dfull[2 * (s // 2) : 2 * (s // 2) + 2, (s % 2) * half : (s % 2 + 1) * half]
    for k in range(1, n):
        target = (me + k) % n
        copy = remote(pbuf.at[target], rbuf.at[k - 1], pot_send.at[k - 1], pot_recv.at[k - 1], target)
        copy.start()
        sent.append(copy)
    summed = pbuf[me]
    for k in range(1, n):
        remote(rbuf.at[k - 1], rbuf.at[k - 1], pot_send.at[k - 1], pot_recv.at[k - 1], partner).wait_recv()
        summed = summed + rbuf[k - 1]
    pot[...] = summed

    wide = tpart.shape[2]
    for order in range(1, TAYLOR + 1):
        for j in range(h):
            where = slice(j * p, (j + 1) * p)
            if order == 1:
                result = s1[:, where]
            else:
                result = lax.dot_general(tbf[...], xbuf[where, :], LAST, preferred_element_type=F32)
            for w in range(2):
                scale = pot[w : w + 1, where] / order
                sc[w * nep : (w + 1) * nep, where] = (result[w * nep : (w + 1) * nep] * scale).astype(BF16)
        last = order == TAYLOR
        for j in range(m // wide):
            result = jnp.dot(sc[...], xbuf[:, j * wide : (j + 1) * wide], preferred_element_type=F32)
            tpart[j] = result
            tsend[order - 1, j] = result.astype(BF16)
            mine = pl.ds(pl.multiple_of((1 - c) * nep, nep), nep) if last else pl.ds(0, 2 * nep)
            view = (order - 1, j, mine)
            copy = remote(
                tsend.at[view], trecv.at[view], term_send.at[order - 1, j], term_recv.at[order - 1, j], partner
            )
            copy.start()
            sent.append(copy)
        own = pl.ds(pl.multiple_of(c * nep, nep), nep)
        for j in range(m // wide):
            where = slice(j * wide, (j + 1) * wide)
            mine = own if last else pl.ds(0, 2 * nep)
            view = trecv.at[order - 1, j, mine]
            remote(view, view, term_send.at[order - 1, j], term_recv.at[order - 1, j], partner).wait_recv()
            total[:, where] += tpart[j, own] + trecv[order - 1, j, own].astype(F32)
            if not last:
                tbf[:, where] = (tpart[j] + trecv[order - 1, j].astype(F32)).astype(BF16)
    for j in range(m // 128):
        out_ref[:, j] = total[0:ne, j * 128 : (j + 1) * 128]
    for copy in sent:
        copy.wait_send()


def fused(orbitals, intersection_inv, factor_rows, factor_rotated, factor_core, fields, n):
    h = n // 2
    p, m = factor_rows.shape
    ne, points = factor_rotated.shape
    nep = -(-ne // 16) * 16
    half = h * p
    walkers = fields.shape[0]
    wide = 512
    vmem = pl.BlockSpec(memory_space=pltpu.VMEM)
    hbm = pl.BlockSpec(memory_space=pl.ANY)
    dma = pltpu.SemaphoreType.DMA
    propagated, force_bias = pl.pallas_call(
        functools.partial(kernel, n),
        out_shape=(
            jax.ShapeDtypeStruct((ne, m // 128, 128), F32),
            jax.ShapeDtypeStruct(fields.shape, F32),
        ),
        in_specs=[hbm, vmem, hbm, hbm, hbm, vmem],
        out_specs=(vmem, vmem),
        scratch_shapes=[
            pltpu.VMEM((half, m), BF16),
            pltpu.VMEM((ne, m // 128, 128), F32),
            pltpu.VMEM((2, 2 * nep, m), BF16),
            pltpu.VMEM((nep, m), F32),
            pltpu.VMEM((ne, points), BF16),
            pltpu.VMEM(factor_core.shape, BF16),
            pltpu.VMEM((2 * nep, half), F32),
            pltpu.VMEM((2 * nep, half), BF16),
            pltpu.VMEM((n, 2, half), F32),
            pltpu.VMEM((walkers, points), F32),
            pltpu.VMEM((n, 2, half), F32),
            pltpu.VMEM((n - 1, 2, half), F32),
            pltpu.VMEM((2, half), F32),
            pltpu.VMEM((m // wide, 2 * nep, wide), F32),
            pltpu.VMEM((TAYLOR, m // wide, 2 * nep, wide), BF16),
            pltpu.VMEM((TAYLOR, m // wide, 2 * nep, wide), BF16),
            pltpu.VMEM((2 * nep, m), BF16),
            pltpu.VMEM((nep, m), F32),
            dma(()),
            dma(()),
            dma(()),
            dma((n,)),
            dma((2, h // 2, 2)),
            dma((2, h // 2, 2)),
            dma((2, h // 2)),
            dma((2, h // 2)),
            dma(()),
            dma(()),
            dma((2, n - 1)),
            dma((2, n - 1)),
            pltpu.SemaphoreType.REGULAR,
            dma((n - 1,)),
            dma((n - 1,)),
            dma((TAYLOR, m // wide)),
            dma((TAYLOR, m // wide)),
        ],
        compiler_params=pltpu.CompilerParams(
            collective_id=0, has_side_effects=True, vmem_limit_bytes=56 * 1024 * 1024
        ),
    )(orbitals.reshape(ne, m // 128, 128), intersection_inv, factor_rows, factor_rotated, factor_core, fields)
    return propagated.reshape(orbitals.shape), force_bias


def density_one(half_green, all_rows, factor_rotated):
    projected = lax.dot_general(half_green, all_rows, LAST, preferred_element_type=F32)
    return jnp.sum(factor_rotated.astype(F32) * projected, axis=0).astype(BF16)


def propagate_one(orbital, potential, all_rows):
    total = orbital
    term = orbital
    for order in range(1, TAYLOR + 1):
        summed = lax.dot_general(term.astype(BF16), all_rows, LAST, preferred_element_type=F32)
        scaled = (summed * potential[None, :] / order).astype(BF16)
        term = jnp.dot(scaled, all_rows, preferred_element_type=F32)
        total = total + term
    return total


def plain(orbitals, intersection_inv, factor_rows, factor_rotated, factor_core, fields):
    walker_count = orbitals.shape[0]
    half_green = jnp.einsum(
        "wij,wjm->wim", intersection_inv, orbitals, precision=lax.Precision.HIGHEST
    ).astype(BF16)
    all_rows = lax.all_gather(factor_rows, "chol", axis=0, tiled=True)
    own_density = lax.map(lambda item: density_one(item, all_rows, factor_rotated), half_green)
    density = lax.all_gather(own_density, "chol", axis=0, tiled=True)
    force_bias = lax.dot_general(density, factor_core, LAST, preferred_element_type=F32)
    shifted = (fields - force_bias).astype(BF16)
    partial_sum = jnp.dot(shifted, factor_core, preferred_element_type=F32)
    summed_all = lax.psum(partial_sum, "chol")
    potential = lax.dynamic_slice_in_dim(
        summed_all, lax.axis_index("chol") * walker_count, walker_count, 0
    )
    propagated = lax.map(lambda pair: propagate_one(pair[0], pair[1], all_rows), (orbitals, potential))
    return (propagated, force_bias)


def solution(mesh):
    n = mesh.shape["chol"]

    def on_device(orbitals, intersection_inv, factor_rows, factor_rotated, factor_core, fields):
        args = (orbitals, intersection_inv, factor_rows, factor_rotated, factor_core, fields)
        rows, m = factor_rows.shape
        if orbitals.shape[0] == 1 and n % 4 == 0 and n > 8 and rows % 256 == 0 and mesh.shape["parts"] == 2 and m % 256 == 0:
            return fused(*args, n)
        return plain(*args)

    in_specs = (
        P(("parts", "chol"), None, None),
        P(("parts", "chol"), None, None),
        P("chol", None),
        P(),
        P("chol", None),
        P("parts", "chol"),
    )
    out_specs = (P(("parts", "chol"), None, None), P("parts", "chol"))
    return jax.shard_map(
        on_device, mesh=mesh, in_specs=in_specs, out_specs=out_specs, check_vma=False
    )
```

profile of v0, /device:TPU:0, one launch (start us, length us, event | category | flops | bytes accessed | tf_op | source)
XLA Modules:
  0.0 72.7 jit_solution(4923104272490490790)
XLA Ops:
  0.6 1.4 %copy.10.inv_ref = f32[1,100,100]{2,1,0:T(8,128)} copy(f32[1,100,100]{2,0,1:T(1,128)} %param.7) | data formatting | bytes 80000 | tf_op args[1]
  2.1 68.2 %shard_map.77 = (f32[100,8,128]{2,1,0:T(8,128)}, f32[16,64]{1,0:T(8,128)}) custom-call(f32[100,8,128]{2,1,0:T(8,128)} %bitcast.2, f32[1,100,100]{2,1,0:T(8,128)} %copy.10.inv_ref, bf16[256,1024]{1,0:T(8,128)(2,1)} %rows_ref.1, bf16[100,4096]{1,0:T(8,128)(2,1)} %rot_ref.1, bf16[64,4096]{1,0:T(8,128)(2,1)} %core_ref.1, f32[16,64]{1,0:T(8,128)} %fields_ref.1), custom_call_target="tpu_custom_call" | custom-call | tf_op jit(solution)/shard_map/pallas_call | solution.py:267
  70.3 0.0 copy-start
  70.3 1.8 %copy.14 = f32[1,100,1024]{2,0,1:T(1,128)} copy(f32[1,100,1024]{2,0,1:T(1,128)} %bitcast.3) | data formatting | bytes 819200
  72.1 0.0 copy-done
  72.1 0.6 copy.15
Async XLA Ops:
  70.3 1.8 %copy-start = (f32[16,64]{1,0:T(8,128)S(1)}, f32[16,64]{1,0:T(8,128)}, u32[]{:S(2)}) copy-start(f32[16,64]{1,0:T(8,128)} %get-tuple-element.13) | copy-start | bytes 12292
where the time goes:
time: 73.2 us; the launch traced here: 72.7 us
  Pallas kernels  68.2 us (93%)
  local copies, waits for them, and re-layouts  3.82 us (5%)
    pallas_call x1, Pallas kernels, fused(): pl.pallas_call(functools.partial(kernel, n), out_shape=(jax.ShapeDtypeStr...  68.2 us
    unnamed x5, local copies, waits for them, and re-layouts  3.82 us

commit v1 on v0

v1 whole, which is shorter than its diff:
```python
import functools

import jax
import jax.numpy as jnp
from jax import lax
from jax.experimental import pallas as pl
from jax.experimental.pallas import tpu as pltpu
from jax.sharding import PartitionSpec as P

TAYLOR = 4
F32, BF16 = jnp.float32, jnp.bfloat16
LAST = (((1,), (1,)), ((), ()))


def kernel(
    n, orb_ref, inv_ref, rows_ref, rot_ref, core_ref, fields_ref, out_ref, fb_ref,
    xbuf, xturn, orb3, lhs, pad, rot, corep, s1, sc, dbuf, dlast, dfull, pbuf, rbuf, pot, tbf, total,
    orb_sem, own_sem, rot_sem, core_sem, ring_send, ring_recv, twin_send, twin_recv, pair_send, pair_recv,
    pass_send, pass_recv, side_send, side_recv, mine_send, mine_recv,
    dens_send, dens_recv, dpair_send, dpair_recv, last_send, last_recv, hello_sem, ready_sem, pot_send, pot_recv,
):
    h = n // 2
    p, m = rows_ref.shape
    ne = orb_ref.shape[0]
    nep = pad.shape[0]
    half = h * p
    side_rows = p * 5 // 256 * 16
    sizes = (side_rows, p - 2 * side_rows)
    here = lax.axis_index("parts")
    starts = (here * side_rows, 2 * side_rows)
    me = lax.axis_index("chol")
    q, c = me // 2, me % 2
    partner = q * 2 + (1 - c)
    r = (1 - q % 2) * (q // 2) + (q % 2) * (h - 1 - q // 2)

    def chip_at(pos):
        pos = (pos + 2 * h) % h
        s = pos // (h // 2)
        return (1 - s) * 2 * pos + s * (2 * (h - 1 - pos) + 1)

    def signal(sem, device):
        pl.semaphore_signal(sem, inc=1, device_id=device, device_id_type=pl.DeviceIdType.MESH)

    barrier = pltpu.get_barrier_semaphore()
    ring = ({"chol": chip_at(r + 1) * 2 + c}, {"chol": chip_at(r - 1) * 2 + c})
    for near in ({"chol": partner}, *ring, {"parts": 1 - here}):
        signal(barrier, near)

    def place(chip, core, first, size):
        return pl.ds(pl.multiple_of(core * half + chip * p + first, 16), size)

    orb_copy = pltpu.make_async_copy(orb_ref, orb3, orb_sem)
    orb_copy.start()
    own_copy = pltpu.make_async_copy(rows_ref, xbuf.at[place(q, c, 0, p)], own_sem)
    own_copy.start()
    rot_copy = pltpu.make_async_copy(rot_ref, rot, rot_sem)
    rot_copy.start()
    core_copies = []
    for s in range(n):
        copy = pltpu.make_async_copy(
            core_ref.at[:, pl.ds(s * p, p)],
            corep.at[:, pl.ds((s % 2) * half + (s // 2) * p, p)],
            core_sem.at[s],
        )
        copy.start()
        core_copies.append(copy)

    pl.semaphore_wait(barrier, 4)
    sent = []

    def remote(src, dst, send, recv, target):
        return pltpu.make_async_remote_copy(
            src_ref=src, dst_ref=dst, send_sem=send, recv_sem=recv,
            device_id={"chol": target}, device_id_type=pl.DeviceIdType.MESH,
        )

    def start(copy):
        copy.start()
        sent.append(copy)

    def rows(way, step, part):
        if step < h // 2:
            return pl.multiple_of(starts[part], 16), sizes[part]
        if part == 1:
            return 2 * side_rows + way * (sizes[1] // 2), sizes[1] // 2
        return pl.multiple_of((way + (1 - 2 * way) * here) * side_rows, 16), side_rows

    def slot(chip, core, way, step, part):
        return xbuf.at[place(chip, core, *rows(way, step, part))]

    def twin(way, step, row):
        view = xbuf.at[place(chip_at(r - (1 - 2 * way) * step), c, row, side_rows)]
        return pltpu.make_async_remote_copy(
            src_ref=view, dst_ref=view, send_sem=twin_send.at[way, step - 1], recv_sem=twin_recv.at[way, step - 1],
            device_id={"parts": 1 - here}, device_id_type=pl.DeviceIdType.MESH,
        )

    def hop(way, step, part):
        sign = 1 - 2 * way
        origin = chip_at(r - sign * (step - 1))
        src = rows_ref.at[pl.ds(*rows(way, step, part))] if step == 1 else slot(origin, c, way, step, part)
        return remote(
            src, slot(origin, c, way, step, part), ring_send.at[way, step - 1, part], ring_recv.at[way, step - 1, part],
            chip_at(r + sign) * 2 + c,
        )

    def arrival(way, step, part):
        sign = 1 - 2 * way
        landed = slot(chip_at(r - sign * step), c, way, step, part)
        return remote(
            landed, landed, ring_send.at[way, step - 1, part], ring_recv.at[way, step - 1, part],
            chip_at(r + sign) * 2 + c,
        )

    def passed(core, way, step, part):
        view = slot(chip_at(r - (1 - 2 * way) * step), core, way, step, part)
        return remote(view, view, pass_send.at[way, step - 1, part], pass_recv.at[way, step - 1, part], partner)

    def aside(core, way, step):
        view = xbuf.at[place(chip_at(r - (1 - 2 * way) * step), core, (1 - here) * side_rows, side_rows)]
        return remote(view, view, side_send.at[way, step - 1], side_recv.at[way, step - 1], partner)

    for part in range(2):
        for way in range(2):
            start(hop(way, 1, part))
    start(remote(rows_ref, xbuf.at[place(q, c, 0, p)], mine_send, mine_recv, partner))
    for near in ring:
        signal(hello_sem.at[0], near)

    pad[...] = jnp.zeros_like(pad)
    orb_copy.wait()
    for j in range(m // 128):
        pad[0:ne, j * 128 : (j + 1) * 128] = orb3[:, j]
    total[...] = pad[...]
    lhs[2] = pad[...].astype(BF16)
    pad[0:ne] = jnp.dot(inv_ref[0], pad[0:ne], preferred_element_type=F32, precision=lax.Precision.HIGHEST)
    lhs[c] = pad[...].astype(BF16)
    start(remote(lhs.at[c], lhs.at[c], pair_send, pair_recv, partner))
    dbuf[c, q] = jnp.zeros(dbuf.shape[2:], BF16)
    own_copy.wait()
    rot_copy.wait()
    for k in range(1, h // 2 - 1):
        pl.semaphore_wait(hello_sem.at[k - 1], 2)
        for near in ring:
            signal(hello_sem.at[k], near)
    remote(lhs.at[1 - c], lhs.at[1 - c], pair_send, pair_recv, partner).wait_recv()

    def turn(where):
        xturn[:, where] = xbuf[where, :].T

    def near_block(chip, last=False):
        where = place(chip, c, 0, p)
        result = lax.dot_general(lhs[...].reshape(3 * nep, m), xbuf[where, :], LAST, preferred_element_type=F32)
        rotated = rot[:, pl.ds(pl.multiple_of((chip * 2 + c) * p, p), p)].astype(F32)
        both = [jnp.sum(rotated * result[w * nep : w * nep + ne], axis=0, keepdims=True) for w in range(2)]
        density = jnp.concatenate(both, axis=0).astype(BF16)
        if last:
            dlast[me] = density
        else:
            dbuf[c, q, :, pl.ds(pl.multiple_of(chip * p, p), p)] = density
        s1[:, pl.ds(pl.multiple_of(c * half + chip * p, p), p)] = result[2 * nep : 3 * nep]

    def far_block(chip):
        where = place(chip, 1 - c, 0, p)
        s1[:, pl.ds(pl.multiple_of((1 - c) * half + chip * p, p), p)] = lax.dot_general(
            lhs[2], xbuf[where, :], LAST, preferred_element_type=F32
        )

    def turns(chip):
        for core in range(2):
            first = pl.multiple_of(core * half + chip * p, p)
            xturn[:, pl.ds(first, p)] = xbuf[pl.ds(first, p), :].T

    def ways(step):
        return range(2 if step < h // 2 - 1 else 1)

    def finish(step):
        for way in ways(step):
            twin(way, step, (1 - here) * side_rows).wait_recv()
            start(aside(c, way, step))
        for way in range(2):
            near_block(chip_at(r - (1 - 2 * way) * step))

    def finish_far(step):
        for way in range(2):
            aside(1 - c, way, step).wait_recv()
            for part in range(2):
                passed(1 - c, way, step, part).wait_recv()
        for way in range(2):
            chip = chip_at(r - (1 - 2 * way) * step)
            far_block(chip)
            turns(chip)

    near_block(q)
    remote(rows_ref, xbuf.at[place(q, 1 - c, 0, p)], mine_send, mine_recv, partner).wait_recv()
    far_block(q)
    turns(q)
    for step in range(1, h // 2):
        for part in range(2):
            for way in (1, 0):
                arrival(way, step, part).wait_recv()
                if step < h // 2 - 1 or (way, part) != (1, 0):
                    start(hop(way, step + 1, part))
                if part == 0:
                    start(twin(way, step, here * side_rows))
                start(passed(c, way, step, part))
        if step == 1:
            pl.semaphore_wait(hello_sem.at[h // 2 - 2], 2)
            signal(ready_sem, {"chol": partner})
        if step == h // 2 - 1:
            twin(1, step, (1 - here) * side_rows).wait_recv()
            start(hop(1, step + 1, 0))
            start(aside(c, 1, step))
        if step > 1:
            finish(step - 1)
            finish_far(step - 1)
    finish(h // 2 - 1)
    pl.semaphore_wait(ready_sem, 1)
    for k in range(1, h):
        target = (q + k) % h * 2 + c
        start(remote(dbuf.at[c, q], dbuf.at[c, q], dens_send.at[k - 1], dens_recv.at[k - 1], target))
    step = h // 2
    for part in range(2):
        for way in (1, 0):
            arrival(way, step, part).wait_recv()
            start(passed(c, way, step, part))
    near_block(chip_at(r - step), True)
    order = sorted(range(1, n), key=lambda k: abs(k - n // 2))
    for k in order:
        start(remote(dlast.at[me], dlast.at[me], last_send.at[k - 1], last_recv.at[k - 1], (me + k) % n))
    for k in range(1, h):
        source = (q + h - k) % h
        view = dbuf.at[c, source]
        remote(view, view, dens_send.at[k - 1], dens_recv.at[k - 1], source * 2 + c).wait_recv()
    start(remote(dbuf.at[c], dbuf.at[c], dpair_send, dpair_recv, partner))
    for copy in core_copies:
        copy.wait()
    finish_far(step - 1)
    remote(dbuf.at[1 - c], dbuf.at[1 - c], dpair_send, dpair_recv, partner).wait_recv()
    for s in range(n):
        dfull[2 * (s // 2) : 2 * (s // 2) + 2, (s % 2) * half : (s % 2 + 1) * half] = dbuf[s % 2, s // 2].astype(F32)
    for way in range(2):
        for part in range(2):
            passed(1 - c, way, step, part).wait_recv()
    far_block(chip_at(r - step))
    turns(chip_at(r - step))
    for k in range(1, n):
        source = (me + n - k) % n
        view = dlast.at[source]
        remote(view, view, last_send.at[k - 1], last_recv.at[k - 1], source).wait_recv()
    for s in range(n):
        chip = s // 2
        pos = chip // 2 if chip % 2 == 0 else h - 1 - chip // 2
        first = (s % 2) * half + chip_at(pos + step) * p
        dfull[2 * chip : 2 * chip + 2, first : first + p] = dlast[s].astype(F32)
    force_bias = lax.dot_general(dfull[...].astype(BF16), corep[...], LAST, preferred_element_type=F32)
    fb_ref[...] = force_bias
    shifted = (fields_ref[...] - force_bias).astype(BF16)
    parts = [
        jnp.dot(shifted, corep[:, side * half : (side + 1) * half], preferred_element_type=F32) for side in range(2)
    ]
    for w in range(n):
        pbuf[w] = jnp.concatenate([part[w : w + 1] for part in parts], axis=0).astype(BF16)
    for k in order:
        target = (me + k) % n
        start(remote(pbuf.at[target], rbuf.at[k - 1], pot_send.at[k - 1], pot_recv.at[k - 1], target))
    summed = pbuf[me].astype(F32)
    for k in range(1, n):
        remote(rbuf.at[k - 1], rbuf.at[k - 1], pot_send.at[k - 1], pot_recv.at[k - 1], partner).wait_recv()
        summed = summed + rbuf[k - 1].astype(F32)
    pot[...] = summed

    wide = 512
    for order in range(1, TAYLOR + 1):
        for j in range(n):
            where = slice(j * p, (j + 1) * p)
            if order == 1:
                result = s1[:, where]
            else:
                result = jnp.dot(tbf[...], xturn[:, where], preferred_element_type=F32)
            scale = pot[j // h : j // h + 1, j % h * p : (j % h + 1) * p] / order
            sc[:, where] = (result * scale).astype(BF16)
        for j in range(m // wide):
            where = slice(j * wide, (j + 1) * wide)
            result = jnp.dot(sc[...], xbuf[:, where], preferred_element_type=F32)
            if order < TAYLOR:
                total[:, where] += result
                tbf[:, where] = result.astype(BF16)
            else:
                for i in range(wide // 128):
                    at = slice(j * wide + i * 128, j * wide + (i + 1) * 128)
                    out_ref[:, j * (wide // 128) + i] = total[0:ne, at] + result[0:ne, i * 128 : (i + 1) * 128]
    for copy in sent:
        copy.wait_send()


def fused(orbitals, intersection_inv, factor_rows, factor_rotated, factor_core, fields, n):
    h = n // 2
    p, m = factor_rows.shape
    ne, points = factor_rotated.shape
    nep = -(-ne // 16) * 16
    half = h * p
    walkers = fields.shape[0]
    vmem = pl.BlockSpec(memory_space=pltpu.VMEM)
    hbm = pl.BlockSpec(memory_space=pl.ANY)
    dma = pltpu.SemaphoreType.DMA
    propagated, force_bias = pl.pallas_call(
        functools.partial(kernel, n),
        out_shape=(
            jax.ShapeDtypeStruct((ne, m // 128, 128), F32),
            jax.ShapeDtypeStruct(fields.shape, F32),
        ),
        in_specs=[hbm, vmem, hbm, hbm, hbm, vmem],
        out_specs=(vmem, vmem),
        scratch_shapes=[
            pltpu.VMEM((points, m), BF16),
            pltpu.VMEM((m, points), BF16),
            pltpu.VMEM((ne, m // 128, 128), F32),
            pltpu.VMEM((3, nep, m), BF16),
            pltpu.VMEM((nep, m), F32),
            pltpu.VMEM((ne, points), BF16),
            pltpu.VMEM(factor_core.shape, BF16),
            pltpu.VMEM((nep, points), F32),
            pltpu.VMEM((nep, points), BF16),
            pltpu.VMEM((2, h, 2, half), BF16),
            pltpu.VMEM((n, 2, p), BF16),
            pltpu.VMEM((walkers, points), F32),
            pltpu.VMEM((n, 2, half), BF16),
            pltpu.VMEM((n - 1, 2, half), BF16),
            pltpu.VMEM((2, half), F32),
            pltpu.VMEM((nep, m), BF16),
            pltpu.VMEM((nep, m), F32),
            dma(()),
            dma(()),
            dma(()),
            dma((n,)),
            dma((2, h // 2, 2)),
            dma((2, h // 2, 2)),
            dma((2, h // 2)),
            dma((2, h // 2)),
            dma(()),
            dma(()),
            dma((2, h // 2, 2)),
            dma((2, h // 2, 2)),
            dma((2, h // 2)),
            dma((2, h // 2)),
            dma(()),
            dma(()),
            dma((h - 1,)),
            dma((h - 1,)),
            dma(()),
            dma(()),
            dma((n - 1,)),
            dma((n - 1,)),
            pltpu.SemaphoreType.REGULAR((h // 2 - 1,)),
            pltpu.SemaphoreType.REGULAR,
            dma((n - 1,)),
            dma((n - 1,)),
        ],
        compiler_params=pltpu.CompilerParams(
            collective_id=0, has_side_effects=True, vmem_limit_bytes=60 * 1024 * 1024
        ),
    )(orbitals.reshape(ne, m // 128, 128), intersection_inv, factor_rows, factor_rotated, factor_core, fields)
    return propagated.reshape(orbitals.shape), force_bias


def density_one(half_green, all_rows, factor_rotated):
    projected = lax.dot_general(half_green, all_rows, LAST, preferred_element_type=F32)
    return jnp.sum(factor_rotated.astype(F32) * projected, axis=0).astype(BF16)


def propagate_one(orbital, potential, all_rows):
    total = orbital
    term = orbital
    for order in range(1, TAYLOR + 1):
        summed = lax.dot_general(term.astype(BF16), all_rows, LAST, preferred_element_type=F32)
        scaled = (summed * potential[None, :] / order).astype(BF16)
        term = jnp.dot(scaled, all_rows, preferred_element_type=F32)
        total = total + term
    return total


def plain(orbitals, intersection_inv, factor_rows, factor_rotated, factor_core, fields):
    walker_count = orbitals.shape[0]
    half_green = jnp.einsum(
        "wij,wjm->wim", intersection_inv, orbitals, precision=lax.Precision.HIGHEST
    ).astype(BF16)
    all_rows = lax.all_gather(factor_rows, "chol", axis=0, tiled=True)
    own_density = lax.map(lambda item: density_one(item, all_rows, factor_rotated), half_green)
    density = lax.all_gather(own_density, "chol", axis=0, tiled=True)
    force_bias = lax.dot_general(density, factor_core, LAST, preferred_element_type=F32)
    shifted = (fields - force_bias).astype(BF16)
    partial_sum = jnp.dot(shifted, factor_core, preferred_element_type=F32)
    summed_all = lax.psum(partial_sum, "chol")
    potential = lax.dynamic_slice_in_dim(
        summed_all, lax.axis_index("chol") * walker_count, walker_count, 0
    )
    propagated = lax.map(lambda pair: propagate_one(pair[0], pair[1], all_rows), (orbitals, potential))
    return (propagated, force_bias)


def solution(mesh):
    n = mesh.shape["chol"]

    def on_device(orbitals, intersection_inv, factor_rows, factor_rotated, factor_core, fields):
        args = (orbitals, intersection_inv, factor_rows, factor_rotated, factor_core, fields)
        rows, m = factor_rows.shape
        if orbitals.shape[0] == 1 and n % 4 == 0 and n > 8 and rows % 256 == 0 and mesh.shape["parts"] == 2 and m % 256 == 0:
            return fused(*args, n)
        return plain(*args)

    in_specs = (
        P(("parts", "chol"), None, None),
        P(("parts", "chol"), None, None),
        P("chol", None),
        P(),
        P("chol", None),
        P("parts", "chol"),
    )
    out_specs = (P(("parts", "chol"), None, None), P("parts", "chol"))
    return jax.shard_map(
        on_device, mesh=mesh, in_specs=in_specs, out_specs=out_specs, check_vma=False
    )
```

time: 73.2 us -> 65 us (0.89)
  Pallas kernels: 68.2 us -> 60.3 us
    pallas_call x1, Pallas kernels: 68.2 us -> 60.3 us  [fused(): pl.pallas_call(functools.partial(kernel, n), out_shape=(jax.ShapeDtypeStr...]
where the time goes in v1:
time: 65 us; the launch traced here: 64.8 us
  Pallas kernels  60.3 us (93%)
  local copies, waits for them, and re-layouts  3.82 us (6%)
  between operations  0.65 us (1%)
    pallas_call x1, Pallas kernels, fused(): pl.pallas_call(functools.partial(kernel, n), out_shape=(jax.ShapeDtypeStr...  60.3 us
    unnamed x5, local copies, waits for them, and re-layouts  3.82 us

profile of v1, /device:TPU:0, one launch (start us, length us, event | category | flops | bytes accessed | tf_op | source)
XLA Modules:
  0.0 64.8 jit_solution(3405991469520918196)
XLA Ops:
  0.6 1.4 %copy.10.inv_ref = f32[1,100,100]{2,1,0:T(8,128)} copy(f32[1,100,100]{2,0,1:T(1,128)} %param.7) | data formatting | bytes 80000 | tf_op args[1]
  2.1 60.3 %shard_map.77 = (f32[100,8,128]{2,1,0:T(8,128)}, f32[16,64]{1,0:T(8,128)}) custom-call(f32[100,8,128]{2,1,0:T(8,128)} %bitcast.2, f32[1,100,100]{2,1,0:T(8,128)} %copy.10.inv_ref, bf16[256,1024]{1,0:T(8,128)(2,1)} %rows_ref.1, bf16[100,4096]{1,0:T(8,128)(2,1)} %rot_ref.1, bf16[64,4096]{1,0:T(8,128)(2,1)} %core_ref.1, f32[16,64]{1,0:T(8,128)} %fields_ref.1), custom_call_target="tpu_custom_call" | custom-call | tf_op jit(solution)/shard_map/pallas_call | solution.py:307
  62.4 0.0 copy-start
  62.4 1.8 %copy.14 = f32[1,100,1024]{2,0,1:T(1,128)} copy(f32[1,100,1024]{2,0,1:T(1,128)} %bitcast.3) | data formatting | bytes 819200
  64.2 0.0 copy-done
  64.2 0.6 copy.15
Async XLA Ops:
  62.4 1.8 %copy-start = (f32[16,64]{1,0:T(8,128)S(1)}, f32[16,64]{1,0:T(8,128)}, u32[]{:S(2)}) copy-start(f32[16,64]{1,0:T(8,128)} %get-tuple-element.13) | copy-start | bytes 12292

commit v2 on v1

v2 whole, which is shorter than its diff:
```python
import functools

import jax
import jax.numpy as jnp
from jax import lax
from jax.experimental import pallas as pl
from jax.experimental.pallas import tpu as pltpu
from jax.sharding import PartitionSpec as P

TAYLOR = 4
F32, BF16 = jnp.float32, jnp.bfloat16
LAST = (((1,), (1,)), ((), ()))


def kernel(
    n, orb_ref, inv_ref, rows_ref, rot_ref, core_ref, fields_ref, out_ref, fb_ref,
    xbuf, xturn, orb3, inv, fields, lhs, pad, rot, corep, s1, sc, dbuf, dlate, dfull, pbuf, rbuf, pot, tbf, total, early,
    orb_sem, inv_sem, fields_sem, own_sem, rot_sem, core_sem, send_sem, ring_recv, twin_recv, pair_recv,
    pass_recv, mine_recv, dens_recv, dpair_recv, late_recv, hello_sem, ready_sem, pot_send, pot_recv,
):
    h = n // 2
    p, m = rows_ref.shape
    ne = orb_ref.shape[0]
    nep = pad.shape[0]
    half = h * p
    side_rows = p * 5 // 256 * 16
    ahead = p // 128 * 16
    offsets, sizes = (0, ahead), (ahead, side_rows - ahead, p - 2 * side_rows)
    here = lax.axis_index("parts")
    me = lax.axis_index("chol")
    q, c = me // 2, me % 2
    partner = q * 2 + (1 - c)
    r = (1 - q % 2) * (q // 2) + (q % 2) * (h - 1 - q // 2)

    def chip_at(pos):
        pos = (pos + 2 * h) % h
        s = pos // (h // 2)
        return (1 - s) * 2 * pos + s * (2 * (h - 1 - pos) + 1)

    def signal(sem, device):
        pl.semaphore_signal(sem, inc=1, device_id=device, device_id_type=pl.DeviceIdType.MESH)

    barrier = pltpu.get_barrier_semaphore()
    ring = ({"chol": chip_at(r + 1) * 2 + c}, {"chol": chip_at(r - 1) * 2 + c})
    for near in ({"chol": partner}, *ring, {"parts": 1 - here}):
        signal(barrier, near)

    def place(chip, core, first, size):
        return pl.ds(pl.multiple_of(core * half + chip * p + first, 16), size)

    own_copy = pltpu.make_async_copy(rows_ref, xbuf.at[place(q, c, 0, p)], own_sem)
    own_copy.start()
    orb_copy = pltpu.make_async_copy(orb_ref, orb3, orb_sem)
    orb_copy.start()
    inv_copy = pltpu.make_async_copy(inv_ref, inv, inv_sem)
    inv_copy.start()
    fields_copy = pltpu.make_async_copy(fields_ref, fields, fields_sem)
    fields_copy.start()
    pl.semaphore_wait(barrier, 4)
    sent = []

    def remote(view, recv, target, dst=None, send=send_sem):
        return pltpu.make_async_remote_copy(
            src_ref=view, dst_ref=view if dst is None else dst, send_sem=send, recv_sem=recv,
            device_id={"chol": target}, device_id_type=pl.DeviceIdType.MESH,
        )

    def arrived(view, recv):
        remote(view, recv, partner).wait_recv()

    def start(copy):
        copy.start()
        sent.append(copy)

    def rows(way, step, part):
        if part < 2:
            side = here if step < h // 2 else way + (1 - 2 * way) * here
            return pl.multiple_of(side * side_rows + offsets[part], 16), sizes[part]
        if step < h // 2:
            return 2 * side_rows, sizes[2]
        return 2 * side_rows + way * (sizes[2] // 2), sizes[2] // 2

    def slot(chip, core, way, step, part):
        return xbuf.at[place(chip, core, *rows(way, step, part))]

    def twin(way, step, part, side):
        row = side * side_rows + offsets[part]
        view = xbuf.at[place(chip_at(r - (1 - 2 * way) * step), c, row, sizes[part])]
        return pltpu.make_async_remote_copy(
            src_ref=view, dst_ref=view,
            send_sem=send_sem, recv_sem=twin_recv.at[way, step - 1, part],
            device_id={"parts": 1 - here}, device_id_type=pl.DeviceIdType.MESH,
        )

    def hop(way, step, part):
        sign = 1 - 2 * way
        view = slot(chip_at(r - sign * (step - 1)), c, way, step, part)
        return remote(view, ring_recv.at[way, step - 1, part], chip_at(r + sign) * 2 + c)

    def arrival(way, step, part):
        arrived(slot(chip_at(r - (1 - 2 * way) * step), c, way, step, part), ring_recv.at[way, step - 1, part])

    def pass_sem(way, step):
        return pass_recv.at[0 if step == h // 2 else way, step - 1]

    def passed(way, step, part):
        return remote(slot(chip_at(r - (1 - 2 * way) * step), c, way, step, part), pass_sem(way, step), partner)

    def aside(way, step, part):
        row = (1 - here) * side_rows + offsets[part]
        view = xbuf.at[place(chip_at(r - (1 - 2 * way) * step), c, row, sizes[part])]
        return remote(view, pass_sem(way, step), partner)

    def passed_block(way, step):
        arrived(xbuf.at[place(chip_at(r - (1 - 2 * way) * step), 1 - c, 0, p)], pass_sem(way, step))

    def across(way, step, part):
        twin(way, step, part, 1 - here).wait_recv()
        start(aside(way, step, part))

    def mine(core):
        return remote(xbuf.at[place(q, core, 0, p)], mine_recv, partner)

    own_copy.wait()
    for part in range(3):
        for way in range(2):
            start(hop(way, 1, part))
    start(mine(c))
    rot_copy = pltpu.make_async_copy(rot_ref, rot, rot_sem)
    rot_copy.start()
    for s in range(n):
        copy = pltpu.make_async_copy(
            core_ref.at[:, pl.ds(s * p, p)],
            corep.at[:, pl.ds((s % 2) * half + (s // 2) * p, p)],
            core_sem,
        )
        copy.start()
    for near in ring:
        signal(hello_sem.at[0], near)

    pad[...] = jnp.zeros_like(pad)
    orb_copy.wait()
    for j in range(m // 128):
        pad[0:ne, j * 128 : (j + 1) * 128] = orb3[:, j]
    total[...] = pad[...]
    lhs[2] = pad[...].astype(BF16)
    inv_copy.wait()
    pad[0:ne] = jnp.dot(inv[:, 0], pad[0:ne], preferred_element_type=F32, precision=lax.Precision.HIGHEST)
    lhs[c] = pad[...].astype(BF16)
    start(remote(lhs.at[c], pair_recv, partner))
    dbuf[c, q] = jnp.zeros(dbuf.shape[2:], BF16)
    rot_copy.wait()
    for k in range(1, h // 2 - 1):
        pl.semaphore_wait(hello_sem.at[k - 1], 2)
        for near in ring:
            signal(hello_sem.at[k], near)
    arrived(lhs.at[1 - c], pair_recv)

    def near_block(chip, late=None):
        where = place(chip, c, 0, p)
        result = lax.dot_general(lhs[...].reshape(3 * nep, m), xbuf[where, :], LAST, preferred_element_type=F32)
        rotated = rot[:, pl.ds(pl.multiple_of((chip * 2 + c) * p, p), p)].astype(F32)
        both = [jnp.sum(rotated * result[w * nep : w * nep + ne], axis=0, keepdims=True) for w in range(2)]
        density = jnp.concatenate(both, axis=0).astype(BF16)
        if late is None:
            dbuf[c, q, :, pl.ds(pl.multiple_of(chip * p, p), p)] = density
        else:
            dlate[me, :, late * p : (late + 1) * p] = density
        s1[:, pl.ds(pl.multiple_of(c * half + chip * p, p), p)] = result[2 * nep : 3 * nep]

    def far_block(chip):
        where = place(chip, 1 - c, 0, p)
        s1[:, pl.ds(pl.multiple_of((1 - c) * half + chip * p, p), p)] = lax.dot_general(
            lhs[2], xbuf[where, :], LAST, preferred_element_type=F32
        )

    def turns(chip):
        for core in range(2):
            first = pl.multiple_of(core * half + chip * p, p)
            xturn[:, pl.ds(first, p)] = xbuf[pl.ds(first, p), :].T

    def near_blocks(step, late=None):
        for way in range(2):
            near_block(chip_at(r - (1 - 2 * way) * step), None if late is None else late + way)

    def finish_far(step):
        for way in range(2):
            passed_block(way, step)
        for way in range(2):
            chip = chip_at(r - (1 - 2 * way) * step)
            far_block(chip)
            turns(chip)

    near_block(q)
    mine(1 - c).wait_recv()
    far_block(q)
    turns(q)
    order = range(n - 1, 0, -1)

    def peer(k):
        flips = [bit for bit in range(k.bit_length()) if k >> bit & 1]
        return me + sum((1 - 2 * (me // 2**bit % 2)) * 2**bit for bit in flips)

    spans = (pl.ds(0, 2 * p), pl.ds(2 * p, p))

    def gather_late(group):
        arrived(dlate.at[pl.ds(0, n - 1), :, spans[group]], late_recv.at[group])
        for s in range(n):
            chip = s // 2
            pos = chip // 2 if chip % 2 == 0 else h - 1 - chip // 2
            for i in ((0, 1), (2,))[group]:
                other = chip_at(pos + ((1 - h // 2), (h // 2 - 1), h // 2)[i])
                first = (s % 2) * half + other * p
                dfull[2 * chip : 2 * chip + 2, first : first + p] = dlate[s, :, i * p : (i + 1) * p].astype(F32)

    final = h // 2 - 1
    for step in range(1, h // 2):
        for part in range(3):
            for way in (1, 0):
                arrival(way, step, part)
                if step < final or way == 0 or part == 2:
                    start(hop(way, step + 1, part))
                if part < 2:
                    start(twin(way, step, part, here))
                start(passed(way, step, part))
            if part == 1 and step > 1:
                for piece in range(2):
                    for way in (1, 0):
                        across(way, step - 1, piece)
                near_blocks(step - 1)
                if step == final:
                    for k in range(1, h):
                        start(remote(dbuf.at[c, q], dens_recv, (q + k) % h * 2 + c))
                    across(1, step, 0)
                    start(hop(1, step + 1, 0))
        if step == final:
            across(1, step, 1)
            start(hop(1, step + 1, 1))
        if step == 1:
            pl.semaphore_wait(hello_sem.at[h // 2 - 2], 2)
            signal(ready_sem, {"chol": partner})
        else:
            finish_far(step - 1)
    for part in range(2):
        across(0, final, part)
    near_blocks(final, 0)
    pl.semaphore_wait(ready_sem, 1)
    for k in order:
        start(remote(dlate.at[me, :, spans[0]], late_recv.at[0], peer(k)))
    step = h // 2
    for turn in range(3):
        for way in (1, 0):
            part = (turn + 2 * way) % 3
            arrival(way, step, part)
            start(passed(way, step, part))
    near_block(chip_at(r - step), 2)
    for k in order:
        start(remote(dlate.at[me, :, spans[1]], late_recv.at[1], peer(k)))
    arrived(dbuf.at[c, pl.ds(0, h - 1)], dens_recv)
    start(remote(dbuf.at[c], dpair_recv, partner))
    fields_copy.wait()
    pltpu.make_async_copy(core_ref, corep, core_sem).wait()
    arrived(dbuf.at[1 - c], dpair_recv)
    for s in range(n):
        dfull[2 * (s // 2) : 2 * (s // 2) + 2, (s % 2) * half : (s % 2 + 1) * half] = dbuf[s % 2, s // 2].astype(F32)
    gather_late(0)
    gather_late(1)
    force_bias = lax.dot_general(dfull[...].astype(BF16), corep[...], LAST, preferred_element_type=F32)
    fb_ref[...] = force_bias
    shifted = (fields[...] - force_bias).astype(BF16)
    run = half // 2
    potentials = []
    for a in range(2):
        parts = [
            jnp.dot(shifted, corep[:, first : first + run], preferred_element_type=F32)
            for first in (a * run, half + a * run)
        ]
        for w in range(n):
            pbuf[a, w] = jnp.concatenate([part[w : w + 1] for part in parts], axis=0).astype(BF16)
        for k in order:
            target = peer(k)
            copy = remote(pbuf.at[a, target], pot_recv.at[a], target, rbuf.at[a, k - 1], pot_send)
            copy.start()
            potentials.append(copy)

    finish_far(final)
    passed_block(0, step)
    far_block(chip_at(r - step))
    turns(chip_at(r - step))
    for copy in sent:
        copy.wait_send()

    wide = 512
    for a in range(2):
        summed = pbuf[a, me].astype(F32)
        arrived(rbuf.at[a], pot_recv.at[a])
        for k in order:
            summed = summed + rbuf[a, k - 1].astype(F32)
        pot[:, a * run : (a + 1) * run] = summed
        for side in range(2):
            where = slice(side * half + a * run, side * half + (a + 1) * run)
            sc[:, where] = (s1[:, where] * summed[side : side + 1]).astype(BF16)
        for j in range(m // wide):
            where = slice(j * wide, (j + 1) * wide)
            result = sum(
                jnp.dot(sc[:, first : first + run], xbuf[first : first + run, where], preferred_element_type=F32)
                for first in (a * run, half + a * run)
            )
            if a == 0:
                early[:, where] = result
            else:
                result = early[:, where] + result
                total[:, where] += result
                tbf[:, where] = result.astype(BF16)
    for order in range(2, TAYLOR + 1):
        for j in range(n):
            where = slice(j * p, (j + 1) * p)
            result = jnp.dot(tbf[...], xturn[:, where], preferred_element_type=F32)
            scale = pot[j // h : j // h + 1, j % h * p : (j % h + 1) * p] / order
            sc[:, where] = (result * scale).astype(BF16)
        for j in range(m // wide):
            where = slice(j * wide, (j + 1) * wide)
            result = jnp.dot(sc[...], xbuf[:, where], preferred_element_type=F32)
            if order < TAYLOR:
                total[:, where] += result
                tbf[:, where] = result.astype(BF16)
            else:
                for i in range(wide // 128):
                    at = slice(j * wide + i * 128, j * wide + (i + 1) * 128)
                    out_ref[:, j * (wide // 128) + i] = total[0:ne, at] + result[0:ne, i * 128 : (i + 1) * 128]
    for copy in potentials:
        copy.wait_send()


def fused(orbitals, intersection_inv, factor_rows, factor_rotated, factor_core, fields, n):
    h = n // 2
    p, m = factor_rows.shape
    ne, points = factor_rotated.shape
    nep = -(-ne // 16) * 16
    half = h * p
    walkers = fields.shape[0]
    vmem = pl.BlockSpec(memory_space=pltpu.VMEM)
    hbm = pl.BlockSpec(memory_space=pl.ANY)
    dma = pltpu.SemaphoreType.DMA
    propagated, force_bias = pl.pallas_call(
        functools.partial(kernel, n),
        out_shape=(pltpu.VMEM((ne, m // 128, 128), F32), pltpu.VMEM(fields.shape, F32)),
        in_specs=[hbm] * 6,
        out_specs=(vmem, vmem),
        scratch_shapes=[
            pltpu.VMEM((points, m), BF16),
            pltpu.VMEM((m, points), BF16),
            pltpu.VMEM((ne, m // 128, 128), F32),
            pltpu.VMEM((ne, 1, ne), F32),
            pltpu.VMEM(fields.shape, F32),
            pltpu.VMEM((3, nep, m), BF16),
            pltpu.VMEM((nep, m), F32),
            pltpu.VMEM((ne, points), BF16),
            pltpu.VMEM(factor_core.shape, BF16),
            pltpu.VMEM((nep, points), F32),
            pltpu.VMEM((nep, points), BF16),
            pltpu.VMEM((2, h, 2, half), BF16),
            pltpu.VMEM((n, 2, 3 * p), BF16),
            pltpu.VMEM((walkers, points), F32),
            pltpu.VMEM((2, n, 2, half // 2), BF16),
            pltpu.VMEM((2, n - 1, 2, half // 2), BF16),
            pltpu.VMEM((2, half), F32),
            pltpu.VMEM((nep, m), BF16),
            pltpu.VMEM((nep, m), F32),
            pltpu.VMEM((nep, m), F32),
            *[dma(())] * 7,
            dma((2, h // 2, 3)),
            dma((2, h // 2 - 1, 2)),
            dma(()),
            dma((2, h // 2)),
            *[dma(())] * 3,
            dma((2,)),
            pltpu.SemaphoreType.REGULAR((h // 2 - 1,)),
            pltpu.SemaphoreType.REGULAR,
            dma(()),
            dma((2,)),
        ],
        compiler_params=pltpu.CompilerParams(
            collective_id=0, has_side_effects=True, vmem_limit_bytes=60 * 1024 * 1024
        ),
    )(orbitals.reshape(ne, m // 128, 128), intersection_inv.reshape(ne, 1, ne), factor_rows, factor_rotated, factor_core, fields)
    pieces = 4
    propagated, force_bias = pl.pallas_call(
        functools.partial(write_out, pieces),
        out_shape=(
            jax.ShapeDtypeStruct(propagated.shape, F32),
            jax.ShapeDtypeStruct(fields.shape, F32),
        ),
        in_specs=[vmem] * 2,
        out_specs=(hbm, hbm),
        scratch_shapes=[dma((pieces + 1,))],
    )(*(pltpu.with_memory_space_constraint(value, pltpu.VMEM) for value in (propagated, force_bias)))
    return propagated.reshape(orbitals.shape), force_bias


def write_out(pieces, propagated, force_bias, out_ref, fb_ref, sem):
    size = propagated.shape[0] // pieces
    copies = [pltpu.make_async_copy(force_bias, fb_ref, sem.at[pieces])]
    for i in range(pieces):
        where = pl.ds(i * size, size)
        copies.append(pltpu.make_async_copy(propagated.at[where], out_ref.at[where], sem.at[i]))
    for copy in copies:
        copy.start()
    for copy in copies:
        copy.wait()


def density_one(half_green, all_rows, factor_rotated):
    projected = lax.dot_general(half_green, all_rows, LAST, preferred_element_type=F32)
    return jnp.sum(factor_rotated.astype(F32) * projected, axis=0).astype(BF16)


def propagate_one(orbital, potential, all_rows):
    total = orbital
    term = orbital
    for order in range(1, TAYLOR + 1):
        summed = lax.dot_general(term.astype(BF16), all_rows, LAST, preferred_element_type=F32)
        scaled = (summed * potential[None, :] / order).astype(BF16)
        term = jnp.dot(scaled, all_rows, preferred_element_type=F32)
        total = total + term
    return total


def plain(orbitals, intersection_inv, factor_rows, factor_rotated, factor_core, fields):
    walker_count = orbitals.shape[0]
    half_green = jnp.einsum(
        "wij,wjm->wim", intersection_inv, orbitals, precision=lax.Precision.HIGHEST
    ).astype(BF16)
    all_rows = lax.all_gather(factor_rows, "chol", axis=0, tiled=True)
    own_density = lax.map(lambda item: density_one(item, all_rows, factor_rotated), half_green)
    density = lax.all_gather(own_density, "chol", axis=0, tiled=True)
    force_bias = lax.dot_general(density, factor_core, LAST, preferred_element_type=F32)
    shifted = (fields - force_bias).astype(BF16)
    partial_sum = jnp.dot(shifted, factor_core, preferred_element_type=F32)
    summed_all = lax.psum(partial_sum, "chol")
    potential = lax.dynamic_slice_in_dim(
        summed_all, lax.axis_index("chol") * walker_count, walker_count, 0
    )
    propagated = lax.map(lambda pair: propagate_one(pair[0], pair[1], all_rows), (orbitals, potential))
    return (propagated, force_bias)


def solution(mesh):
    n = mesh.shape["chol"]

    def on_device(orbitals, intersection_inv, factor_rows, factor_rotated, factor_core, fields):
        args = (orbitals, intersection_inv, factor_rows, factor_rotated, factor_core, fields)
        rows, m = factor_rows.shape
        if orbitals.shape[0] == 1 and n & (n - 1) == 0 and n > 8 and rows % 256 == 0 and mesh.shape["parts"] == 2 and m % 256 == 0:
            return fused(*args, n)
        return plain(*args)

    in_specs = (
        P(("parts", "chol"), None, None),
        P(("parts", "chol"), None, None),
        P("chol", None),
        P(),
        P("chol", None),
        P("parts", "chol"),
    )
    out_specs = (P(("parts", "chol"), None, None), P("parts", "chol"))
    return jax.shard_map(
        on_device, mesh=mesh, in_specs=in_specs, out_specs=out_specs, check_vma=False
    )
```

time: 65 us -> 56.4 us (0.87)
  Pallas kernels: 60.3 us -> 55.5 us
  local copies, waits for them, and re-layouts: 3.82 us -> 0 us
    pallas_call x1 -> x2, Pallas kernels: 60.3 us -> 55.5 us  [the longest x1 54.7 us: fused(): pl.pallas_call(functools.partial(kernel, n), out_shape=(pltpu.VMEM((ne, m...]
    unnamed x5 -> x0, local copies, waits for them, and re-layouts: 3.82 us -> none
where the time goes in v2:
time: 56.4 us; the launch traced here: 56.3 us
  Pallas kernels  55.5 us (98%)
  between operations  0.8 us (1%)
    pallas_call x1, Pallas kernels, fused(): pl.pallas_call(functools.partial(kernel, n), out_shape=(pltpu.VMEM((ne, m...  54.7 us

profile of v2, /device:TPU:0, one launch (start us, length us, event | category | flops | bytes accessed | tf_op | source)
XLA Modules:
  0.0 56.3 jit_solution(7899631282460563858)
XLA Ops:
  0.6 54.7 %shard_map.77 = (f32[100,8,128]{2,1,0:T(8,128)S(1)}, f32[16,64]{1,0:T(8,128)S(1)}) custom-call(f32[100,8,128]{2,1,0:T(8,128)} %bitcast.3, f32[100,1,100]{2,1,0:T(1,128)} %bitcast.4, bf16[256,1024]{1,0:T(8,128)(2,1)} %rows_ref.1, bf16[100,4096]{1,0:T(8,128)(2,1)} %rot_ref.1, bf16[64,4096]{1,0:T(8,128)(2,1)} %core_ref.1, f32[16,64]{1,0:T(8,128)} %fields_ref.1), custom_call_target="tpu_custom_call" | custom-call | tf_op jit(solution)/shard_map/pallas_call | solution.py:345
  55.3 0.8 %shard_map.78 = (f32[100,8,128]{2,1,0:T(8,128)}, f32[16,64]{1,0:T(8,128)}) custom-call(f32[100,8,128]{2,1,0:T(8,128)S(1)} %get-tuple-element.6.propagated, f32[16,64]{1,0:T(8,128)S(1)} %get-tuple-element.7.force_bias), custom_call_target="tpu_custom_call" | custom-call | tf_op jit(solution)/shard_map/pallas_call | solution.py:388

commit v3 on v2

v3 whole, which is shorter than its diff:
```python
import functools

import jax
import jax.numpy as jnp
from jax import lax
from jax.experimental import pallas as pl
from jax.experimental.pallas import tpu as pltpu
from jax.sharding import PartitionSpec as P

TAYLOR = 4
F32, BF16 = jnp.float32, jnp.bfloat16
LAST = (((1,), (1,)), ((), ()))


def kernel(
    n, orb_ref, inv_ref, rows_ref, rot_ref, core_ref, fields_ref, out_ref, fb_ref,
    xbuf, xturn, orb3, inv, fields, lhs, pad, rot, corep, s1, sc, dbuf, dlate, dfull, fpart, fother, pbuf, rbuf, pot,
    tbf, total, early,
    orb_sem, inv_sem, fields_sem, own_sem, rot_sem, core_sem, send_sem, pair_recv, guest_recv, share_recv, mine_recv,
    dens_recv, dpair_recv, swap_recv, pot_send, ready_sem, ring_recv, twin_recv, pass_recv, late_recv, pot_recv, hello_sem,
):
    h = n // 2
    p, m = rows_ref.shape
    ne = orb_ref.shape[0]
    nep = pad.shape[0]
    hp = p // 2
    run = h * hp
    side = n * hp
    shared = hp // 2
    size = shared // 2
    final = h // 2
    here = lax.axis_index("parts")
    me = lax.axis_index("chol")
    q, c = me // 2, me % 2
    partner = q * 2 + (1 - c)
    r = (1 - q % 2) * (q // 2) + (q % 2) * (h - 1 - q // 2)
    halves = (here, 1 - here)

    pieces = ((0, 0), (0, size), (0, 2 * size), (0, 3 * size), (1, 2 * size), (1, 3 * size))

    def chip_at(pos):
        pos = (pos + 2 * h) % h
        s = pos // (h // 2)
        return (1 - s) * 2 * pos + s * (2 * (h - 1 - pos) + 1)

    def signal(sem, device):
        pl.semaphore_signal(sem, inc=1, device_id=device, device_id_type=pl.DeviceIdType.MESH)

    barrier = pltpu.get_barrier_semaphore()
    ring = ({"chol": chip_at(r + 1) * 2 + c}, {"chol": chip_at(r - 1) * 2 + c})
    for near in ({"chol": partner}, *ring, {"parts": 1 - here}):
        signal(barrier, near)

    def place(second, core, chip, first, size):
        return pl.ds(pl.multiple_of(second * side + core * run + chip * hp + first, 16), size)

    def columns(second, core, chip):
        return pl.ds(pl.multiple_of(second * side + core * run + chip * hp, hp), hp)

    for second in range(2):
        pltpu.make_async_copy(
            rows_ref.at[pl.ds(pl.multiple_of(halves[second] * hp, hp), hp)], xbuf.at[place(second, c, q, 0, hp)], own_sem
        ).start()
    orb_copy = pltpu.make_async_copy(orb_ref, orb3, orb_sem)
    orb_copy.start()
    inv_copy = pltpu.make_async_copy(inv_ref, inv, inv_sem)
    inv_copy.start()
    fields_copy = pltpu.make_async_copy(fields_ref, fields, fields_sem)
    fields_copy.start()

    pl.semaphore_wait(barrier, 4)
    sent = []

    def remote(view, recv, target, dst=None, send=send_sem):
        return pltpu.make_async_remote_copy(
            src_ref=view, dst_ref=view if dst is None else dst, send_sem=send, recv_sem=recv,
            device_id=target if isinstance(target, dict) else {"chol": target}, device_id_type=pl.DeviceIdType.MESH,
        )

    def arrived(view, recv):
        remote(view, recv, partner).wait_recv()

    def start(copy):
        copy.start()
        sent.append(copy)

    def from_chip(way, step):
        return chip_at(r - (1 - 2 * way) * step)

    def slot(chip, kind):
        second, first = pieces[kind]
        return xbuf.at[place(second, c, chip, first, size)]

    def hop(way, step, kind):
        return remote(slot(from_chip(way, step - 1), kind), ring_recv.at[way, step - 1, kind], dict(ring[way]))

    def pass_sem(second, way, step):
        return pass_recv.at[second, 0 if step == final else way, step - 1]

    def take(way, step, kind):
        view = slot(from_chip(way, step), kind)
        arrived(view, ring_recv.at[way, step - 1, kind])
        if step + 1 < final or (step + 1 == final and way == kind % 2):
            start(hop(way, step + 1, kind))
        second, first = pieces[kind]
        if kind < 2:
            other = xbuf.at[place(1, c, from_chip(way, step), first, size)]
            start(remote(view, twin_recv.at[0 if step == final else way, step - 1], {"parts": 1 - here}, other))
        start(remote(view, pass_sem(second, way, step), partner))

    def take_both(step, *kinds):
        for kind in kinds:
            for way in (1, 0):
                if step < final or way == kind % 2:
                    take(way, step, kind)

    def across(way, step):
        view = xbuf.at[place(1, c, from_chip(way, step), 0, shared)]
        arrived(view, twin_recv.at[way, step - 1])
        start(remote(view, pass_sem(1, way, step), partner))

    pltpu.make_async_copy(rows_ref, xbuf.at[pl.ds(0, p)], own_sem).wait()
    for kind in range(4):
        for way in range(2):
            start(hop(way, 1, kind))
    for second in range(2):
        start(remote(xbuf.at[place(second, c, q, 0, hp)], mine_recv, partner))
    for chip in range(h):
        first = pl.multiple_of((chip * 2 + c) * p + here * hp, hp)
        pltpu.make_async_copy(rot_ref.at[:, pl.ds(first, hp)], rot.at[:, pl.ds(chip * hp, hp)], rot_sem).start()
    for second in range(2):
        for s in range(n):
            first = pl.multiple_of(s * p + halves[second] * hp, hp)
            pltpu.make_async_copy(
                core_ref.at[:, pl.ds(first, hp)],
                corep.at[:, pl.ds(second * side + (s % 2) * run + (s // 2) * hp, hp)],
                core_sem,
            ).start()
    for near in ring:
        signal(hello_sem.at[0], near)

    pad[...] = jnp.zeros_like(pad)
    orb_copy.wait()
    for j in range(m // 128):
        pad[0:ne, j * 128 : (j + 1) * 128] = orb3[:, j]
    total[...] = pad[...]
    lhs[4] = pad[...].astype(BF16)
    inv_copy.wait()
    pad[0:ne] = jnp.dot(inv[:, 0], pad[0:ne], preferred_element_type=F32, precision=lax.Precision.HIGHEST)
    lhs[c] = pad[...].astype(BF16)
    start(remote(lhs.at[c], guest_recv, {"parts": 1 - here}, lhs.at[2 + c]))
    start(remote(lhs.at[c], pair_recv, partner))
    dbuf[c, q] = jnp.zeros(dbuf.shape[2:], BF16)
    for k in range(1, h // 2 - 1):
        pl.semaphore_wait(hello_sem.at[k - 1], 2)
        for near in ring:
            signal(hello_sem.at[k], near)
    arrived(lhs.at[1 - c], pair_recv)
    pltpu.make_async_copy(rot_ref.at[:, pl.ds(0, run)], rot, rot_sem).wait()

    def turn(second, core, chip):
        xturn[:, columns(second, core, chip)] = xbuf[place(second, core, chip, 0, hp), :].T

    def near_block(chip, late=None):
        result = lax.dot_general(
            lhs[...].reshape(5 * nep, m), xbuf[place(0, c, chip, 0, hp), :], LAST, preferred_element_type=F32
        )
        rotated = rot[:, pl.ds(pl.multiple_of(chip * hp, hp), hp)].astype(F32)
        each = [jnp.sum(rotated * result[w * nep : w * nep + ne], axis=0, keepdims=True) for w in range(4)]
        density = jnp.concatenate(each, axis=0).astype(BF16)
        if late is None:
            dbuf[c, q, :, pl.ds(pl.multiple_of(chip * hp, hp), hp)] = density
        else:
            dlate[me, :, late * hp : (late + 1) * hp] = density
        s1[:, columns(0, c, chip)] = result[4 * nep : 5 * nep]

    def block(second, core, chip):
        s1[:, columns(second, core, chip)] = lax.dot_general(
            lhs[4], xbuf[place(second, core, chip, 0, hp), :], LAST, preferred_element_type=F32
        )
        turn(second, core, chip)

    def ways(step):
        return range(2 if step < final else 1)

    def near_blocks(step, late=None):
        for way in ways(step):
            near_block(from_chip(way, step), None if late is None else late + way)

    def far_blocks(second, step):
        for way in ways(step):
            arrived(xbuf.at[place(second, 1 - c, from_chip(way, step), 0, hp)], pass_sem(second, way, step))
            block(second, 1 - c, from_chip(way, step))

    def turns(step):
        for way in ways(step):
            turn(0, c, from_chip(way, step))

    def second_blocks(step):
        for way in ways(step):
            block(1, c, from_chip(way, step))
        far_blocks(1, step)

    order = range(n - 1, 0, -1)

    def peer(k):
        flips = [bit for bit in range(k.bit_length()) if k >> bit & 1]
        return me + sum((1 - 2 * (me // 2**bit % 2)) * 2**bit for bit in flips)

    spans = (pl.ds(0, 2 * hp), pl.ds(2 * hp, hp))

    def send_late(group):
        for k in order:
            start(remote(dlate.at[me, :, spans[group]], late_recv.at[group], peer(k)))

    def spread_rows(value, chip, where):
        for part in range(2):
            dfull[part * n + 2 * chip : part * n + 2 * chip + 2, where] = value[2 * part : 2 * part + 2].astype(F32)

    def gather_late(group):
        arrived(dlate.at[pl.ds(0, n - 1), :, spans[group]], late_recv.at[group])
        for s in range(n):
            chip = s // 2
            pos = chip // 2 if chip % 2 == 0 else h - 1 - chip // 2
            for i in ((0, 1), (2,))[group]:
                other = chip_at(pos + (1 - final, final - 1, final)[i])
                first = (s % 2) * run + other * hp
                spread_rows(dlate[s, :, i * hp : (i + 1) * hp], chip, slice(first, first + hp))

    block(1, c, q)
    arrived(xbuf.at[pl.ds(0, p)], mine_recv)
    block(0, 1 - c, q)
    block(1, 1 - c, q)
    take_both(1, 0, 1, 2, 3)
    pl.semaphore_wait(hello_sem.at[h // 2 - 2], 2)
    signal(ready_sem, {"chol": partner})
    arrived(lhs.at[2 + c], guest_recv)
    start(remote(lhs.at[2 + c], share_recv, partner))
    arrived(lhs.at[3 - c], share_recv)
    near_block(q)
    turn(0, c, q)
    for step in range(2, final):
        take_both(step, 0, 1)
        near_blocks(step - 1)
        if step == final - 1:
            for k in range(1, h):
                start(remote(dbuf.at[c, q], dens_recv, (q + k) % h * 2 + c))
        take_both(step, 2)
        if step < final - 1:
            far_blocks(0, step - 1)
            turns(step - 1)
        take_both(step, 3)
    for kind in (4, 5):
        for way in range(2):
            start(hop(way, 1, kind))
    near_blocks(final - 1, 0)
    pl.semaphore_wait(ready_sem, 1)
    send_late(0)
    for way in range(2):
        across(way, 1)
    far_blocks(0, final - 2)
    turns(final - 2)
    take_both(final, 0, 1, 2, 3)
    near_blocks(final, 2)
    send_late(1)
    for way in range(2):
        across(way, 2)
    take_both(1, 4)
    far_blocks(0, final - 1)
    turns(final - 1)
    take_both(1, 5)
    arrived(dbuf.at[c, pl.ds(0, h - 1)], dens_recv)
    start(remote(dbuf.at[c], dpair_recv, partner))
    fields_copy.wait()
    pltpu.make_async_copy(core_ref, corep, core_sem).wait()
    second_blocks(1)
    arrived(dbuf.at[1 - c], dpair_recv)
    for s in range(n):
        spread_rows(dbuf[s % 2, s // 2], s // 2, slice((s % 2) * run, (s % 2 + 1) * run))
    gather_late(0)
    take_both(2, 4)
    gather_late(1)
    partial = lax.dot_general(dfull[...].astype(BF16), corep[:, 0:side], LAST, preferred_element_type=F32)
    fpart[...] = partial[n : 2 * n]
    start(remote(fpart, swap_recv, {"parts": 1 - here}, fother))
    take_both(2, 5)
    for step in range(3, final):
        for way in range(2):
            across(way, step)
    arrived(fother, swap_recv)
    force_bias = partial[0:n] + fother[...]
    fb_ref[...] = force_bias
    shifted = (fields[...] - force_bias).astype(BF16)
    potentials = []
    for a in range(2):
        parts = [
            jnp.dot(shifted, corep[:, first : first + run], preferred_element_type=F32)
            for first in (a * side, a * side + run)
        ]
        for w in range(n):
            pbuf[a, w] = jnp.concatenate([part[w : w + 1] for part in parts], axis=0).astype(BF16)
        for k in order:
            target = peer(k)
            copy = remote(pbuf.at[a, target], pot_recv.at[a], target, rbuf.at[a, k - 1], pot_send)
            copy.start()
            potentials.append(copy)
    take_both(3, 4)
    second_blocks(2)
    take_both(3, 5)
    far_blocks(0, final)
    turns(final)
    across(0, final)
    take_both(final, 4, 5)
    second_blocks(3)
    second_blocks(final)
    for copy in sent:
        copy.wait_send()

    wide = 512
    for a in range(2):
        half = slice(a * side, (a + 1) * side)
        summed = pbuf[a, me].astype(F32)
        arrived(rbuf.at[a], pot_recv.at[a])
        for k in order:
            summed = summed + rbuf[a, k - 1].astype(F32)
        pot[a] = summed
        for core in range(2):
            where = slice(a * side + core * run, a * side + (core + 1) * run)
            sc[:, where] = (s1[:, where] * summed[core : core + 1]).astype(BF16)
        for j in range(m // wide):
            where = slice(j * wide, (j + 1) * wide)
            result = jnp.dot(sc[:, half], xbuf[half, where], preferred_element_type=F32)
            if a == 0:
                early[:, where] = result
            else:
                result = early[:, where] + result
                total[:, where] += result
                tbf[:, where] = result.astype(BF16)
    for order in range(2, TAYLOR + 1):
        for j in range(n):
            where = slice(j * p, (j + 1) * p)
            result = jnp.dot(tbf[...], xturn[:, where], preferred_element_type=F32)
            a, core, first = j // h, j % h * 2 // h, j % (h // 2) * p
            scale = pot[a, core : core + 1, first : first + p] / order
            sc[:, where] = (result * scale).astype(BF16)
        for j in range(m // wide):
            where = slice(j * wide, (j + 1) * wide)
            result = jnp.dot(sc[...], xbuf[:, where], preferred_element_type=F32)
            if order < TAYLOR:
                total[:, where] += result
                tbf[:, where] = result.astype(BF16)
            else:
                for i in range(wide // 128):
                    at = slice(j * wide + i * 128, j * wide + (i + 1) * 128)
                    out_ref[:, j * (wide // 128) + i] = total[0:ne, at] + result[0:ne, i * 128 : (i + 1) * 128]
    for copy in potentials:
        copy.wait_send()


def fused(orbitals, intersection_inv, factor_rows, factor_rotated, factor_core, fields, n):
    h = n // 2
    p, m = factor_rows.shape
    ne, points = factor_rotated.shape
    nep = -(-ne // 16) * 16
    hp = p // 2
    run, side = h * hp, n * hp
    vmem = pl.BlockSpec(memory_space=pltpu.VMEM)
    hbm = pl.BlockSpec(memory_space=pl.ANY)
    dma = pltpu.SemaphoreType.DMA
    propagated, force_bias = pl.pallas_call(
        functools.partial(kernel, n),
        out_shape=(pltpu.VMEM((ne, m // 128, 128), F32), pltpu.VMEM(fields.shape, F32)),
        in_specs=[hbm] * 6,
        out_specs=(vmem, vmem),
        scratch_shapes=[
            pltpu.VMEM((points, m), BF16),
            pltpu.VMEM((m, points), BF16),
            pltpu.VMEM((ne, m // 128, 128), F32),
            pltpu.VMEM((ne, 1, ne), F32),
            pltpu.VMEM(fields.shape, F32),
            pltpu.VMEM((5, nep, m), BF16),
            pltpu.VMEM((nep, m), F32),
            pltpu.VMEM((ne, run), BF16),
            pltpu.VMEM(factor_core.shape, BF16),
            pltpu.VMEM((nep, points), F32),
            pltpu.VMEM((nep, points), BF16),
            pltpu.VMEM((2, h, 4, run), BF16),
            pltpu.VMEM((n, 4, 3 * hp), BF16),
            pltpu.VMEM((2 * n, side), F32),
            pltpu.VMEM(fields.shape, F32),
            pltpu.VMEM(fields.shape, F32),
            pltpu.VMEM((2, n, 2, run), BF16),
            pltpu.VMEM((2, n - 1, 2, run), BF16),
            pltpu.VMEM((2, 2, run), F32),
            pltpu.VMEM((nep, m), BF16),
            pltpu.VMEM((nep, m), F32),
            pltpu.VMEM((nep, m), F32),
            *[dma(())] * 15,
            pltpu.SemaphoreType.REGULAR,
            dma((2, h // 2, 6)),
            dma((2, h // 2)),
            dma((2, 2, h // 2)),
            dma((2,)),
            dma((2,)),
            pltpu.SemaphoreType.REGULAR((h // 2 - 1,)),
        ],
        compiler_params=pltpu.CompilerParams(
            collective_id=0, has_side_effects=True, vmem_limit_bytes=60 * 1024 * 1024
        ),
    )(
        orbitals.reshape(ne, m // 128, 128), intersection_inv.reshape(ne, 1, ne),
        factor_rows, factor_rotated, factor_core, fields,
    )
    pieces = 4
    propagated, force_bias = pl.pallas_call(
        functools.partial(write_out, pieces),
        out_shape=(
            jax.ShapeDtypeStruct(propagated.shape, F32),
            jax.ShapeDtypeStruct(fields.shape, F32),
        ),
        in_specs=[vmem] * 2,
        out_specs=(hbm, hbm),
        scratch_shapes=[dma((pieces + 1,))],
    )(*(pltpu.with_memory_space_constraint(value, pltpu.VMEM) for value in (propagated, force_bias)))
    return propagated.reshape(orbitals.shape), force_bias


def write_out(pieces, propagated, force_bias, out_ref, fb_ref, sem):
    size = propagated.shape[0] // pieces
    copies = [pltpu.make_async_copy(force_bias, fb_ref, sem.at[pieces])]
    for i in range(pieces):
        where = pl.ds(i * size, size)
        copies.append(pltpu.make_async_copy(propagated.at[where], out_ref.at[where], sem.at[i]))
    for copy in copies:
        copy.start()
    for copy in copies:
        copy.wait()


def density_one(half_green, all_rows, factor_rotated):
    projected = lax.dot_general(half_green, all_rows, LAST, preferred_element_type=F32)
    return jnp.sum(factor_rotated.astype(F32) * projected, axis=0).astype(BF16)


def propagate_one(orbital, potential, all_rows):
    total = orbital
    term = orbital
    for order in range(1, TAYLOR + 1):
        summed = lax.dot_general(term.astype(BF16), all_rows, LAST, preferred_element_type=F32)
        scaled = (summed * potential[None, :] / order).astype(BF16)
        term = jnp.dot(scaled, all_rows, preferred_element_type=F32)
        total = total + term
    return total


def plain(orbitals, intersection_inv, factor_rows, factor_rotated, factor_core, fields):
    walker_count = orbitals.shape[0]
    half_green = jnp.einsum(
        "wij,wjm->wim", intersection_inv, orbitals, precision=lax.Precision.HIGHEST
    ).astype(BF16)
    all_rows = lax.all_gather(factor_rows, "chol", axis=0, tiled=True)
    own_density = lax.map(lambda item: density_one(item, all_rows, factor_rotated), half_green)
    density = lax.all_gather(own_density, "chol", axis=0, tiled=True)
    force_bias = lax.dot_general(density, factor_core, LAST, preferred_element_type=F32)
    shifted = (fields - force_bias).astype(BF16)
    partial_sum = jnp.dot(shifted, factor_core, preferred_element_type=F32)
    summed_all = lax.psum(partial_sum, "chol")
    potential = lax.dynamic_slice_in_dim(
        summed_all, lax.axis_index("chol") * walker_count, walker_count, 0
    )
    propagated = lax.map(lambda pair: propagate_one(pair[0], pair[1], all_rows), (orbitals, potential))
    return (propagated, force_bias)


def solution(mesh):
    n = mesh.shape["chol"]

    def on_device(orbitals, intersection_inv, factor_rows, factor_rotated, factor_core, fields):
        args = (orbitals, intersection_inv, factor_rows, factor_rotated, factor_core, fields)
        rows, m = factor_rows.shape
        if orbitals.shape[0] == 1 and n == 16 and rows % 256 == 0 and mesh.shape["parts"] == 2 and m % 512 == 0:
            return fused(*args, n)
        return plain(*args)

    in_specs = (
        P(("parts", "chol"), None, None),
        P(("parts", "chol"), None, None),
        P("chol", None),
        P(),
        P("chol", None),
        P("parts", "chol"),
    )
    out_specs = (P(("parts", "chol"), None, None), P("parts", "chol"))
    return jax.shard_map(
        on_device, mesh=mesh, in_specs=in_specs, out_specs=out_specs, check_vma=False
    )
```

time: 56.4 us -> 54.2 us (0.961)
  Pallas kernels: 55.5 us -> 53.3 us
    pallas_call x1, Pallas kernels: 54.7 us -> 52.5 us  [fused(): pl.pallas_call(functools.partial(kernel, n), out_shape=(pltpu.VMEM((ne, m...]
where the time goes in v3:
time: 54.2 us; the launch traced here: 54.1 us
  Pallas kernels  53.3 us (98%)
  between operations  0.8 us (1%)
    pallas_call x1, Pallas kernels, fused(): pl.pallas_call(functools.partial(kernel, n), out_shape=(pltpu.VMEM((ne, m...  52.5 us

profile of v3, /device:TPU:0, one launch (start us, length us, event | category | flops | bytes accessed | tf_op | source)
XLA Modules:
  0.0 54.1 jit_solution(6378871199682747925)
XLA Ops:
  0.6 52.5 %shard_map.77 = (f32[100,8,128]{2,1,0:T(8,128)S(1)}, f32[16,64]{1,0:T(8,128)S(1)}) custom-call(f32[100,8,128]{2,1,0:T(8,128)} %bitcast.3, f32[100,1,100]{2,1,0:T(1,128)} %bitcast.4, bf16[256,1024]{1,0:T(8,128)(2,1)} %rows_ref.1, bf16[100,4096]{1,0:T(8,128)(2,1)} %rot_ref.1, bf16[64,4096]{1,0:T(8,128)(2,1)} %core_ref.1, f32[16,64]{1,0:T(8,128)} %fields_ref.1), custom_call_target="tpu_custom_call" | custom-call | tf_op jit(solution)/shard_map/pallas_call | solution.py:370
  53.1 0.8 %shard_map.78 = (f32[100,8,128]{2,1,0:T(8,128)}, f32[16,64]{1,0:T(8,128)}) custom-call(f32[100,8,128]{2,1,0:T(8,128)S(1)} %get-tuple-element.6.propagated, f32[16,64]{1,0:T(8,128)S(1)} %get-tuple-element.7.force_bias), custom_call_target="tpu_custom_call" | custom-call | tf_op jit(solution)/shard_map/pallas_call | solution.py:415

commit v4 on v3

--- a/solution.py
+++ b/solution.py
@@ -14,10 +14,10 @@
 
 def kernel(
     n, orb_ref, inv_ref, rows_ref, rot_ref, core_ref, fields_ref, out_ref, fb_ref,
-    xbuf, xturn, orb3, inv, fields, lhs, pad, rot, corep, s1, sc, dbuf, dlate, dfull, fpart, fother, pbuf, rbuf, pot,
+    xbuf, xturn, orb3, inv, fields, lhs, pad, rot, corep, s1, sc, dbuf, dlast, dguest, dfull, dtail, fpart, fother, pbuf, rbuf, pot,
     tbf, total, early,
     orb_sem, inv_sem, fields_sem, own_sem, rot_sem, core_sem, send_sem, pair_recv, guest_recv, share_recv, mine_recv,
-    dens_recv, dpair_recv, swap_recv, pot_send, ready_sem, ring_recv, twin_recv, pass_recv, late_recv, pot_recv, hello_sem,
+    dens_recv, dpair_recv, swap_recv, pot_send, ready_sem, all_sem, ring_recv, twin_recv, extra_recv, pass_recv, last_recv, pot_recv, hello_sem,
 ):
     h = n // 2
     p, m = rows_ref.shape
@@ -97,27 +97,45 @@
     def pass_sem(second, way, step):
         return pass_recv.at[second, 0 if step == final else way, step - 1]
 
+    def travels(way, step, kind):
+        if step < final:
+            return (step, kind) != (final - 1, 5)
+        return step == final and kind < 4 and way == kind % 2
+
     def take(way, step, kind):
         view = slot(from_chip(way, step), kind)
         arrived(view, ring_recv.at[way, step - 1, kind])
-        if step + 1 < final or (step + 1 == final and way == kind % 2):
+        if travels(way, step + 1, kind):
             start(hop(way, step + 1, kind))
-        second, first = pieces[kind]
-        if kind < 2:
-            other = xbuf.at[place(1, c, from_chip(way, step), first, size)]
-            start(remote(view, twin_recv.at[0 if step == final else way, step - 1], {"parts": 1 - here}, other))
-        start(remote(view, pass_sem(second, way, step), partner))
+        if kind < 2 and step < final:
+            share(way, step, kind)
+        start(remote(view, pass_sem(pieces[kind][0], way, step), partner))
+
+    def share(way, step, kind):
+        chip = from_chip(way, step)
+        other = xbuf.at[place(1, c, chip, pieces[kind][1], size)]
+        if step == final:
+            arrives = twin_recv.at[kind // 2, step - 1]
+        else:
+            arrives = twin_recv.at[way, step - 1] if kind < 2 else extra_recv.at[way]
+        start(remote(slot(chip, kind), arrives, {"parts": 1 - here}, other))
 
     def take_both(step, *kinds):
         for kind in kinds:
             for way in (1, 0):
-                if step < final or way == kind % 2:
+                if travels(way, step, kind):
                     take(way, step, kind)
 
     def across(way, step):
-        view = xbuf.at[place(1, c, from_chip(way, step), 0, shared)]
+        first = way * shared if step == final else 0
+        view = xbuf.at[place(1, c, from_chip(way, step), first, shared)]
         arrived(view, twin_recv.at[way, step - 1])
         start(remote(view, pass_sem(1, way, step), partner))
+
+    def across_extra(way):
+        view = xbuf.at[place(1, c, from_chip(way, final - 1), 3 * size, size)]
+        arrived(view, extra_recv.at[way])
+        start(remote(view, pass_sem(1, way, final - 1), partner))
 
     pltpu.make_async_copy(rows_ref, xbuf.at[pl.ds(0, p)], own_sem).wait()
     for kind in range(4):
@@ -151,6 +169,7 @@
     start(remote(lhs.at[c], guest_recv, {"parts": 1 - here}, lhs.at[2 + c]))
     start(remote(lhs.at[c], pair_recv, partner))
     dbuf[c, q] = jnp.zeros(dbuf.shape[2:], BF16)
+    dtail[...] = jnp.zeros_like(dtail)
     for k in range(1, h // 2 - 1):
         pl.semaphore_wait(hello_sem.at[k - 1], 2)
         for near in ring:
@@ -161,17 +180,18 @@
     def turn(second, core, chip):
         xturn[:, columns(second, core, chip)] = xbuf[place(second, core, chip, 0, hp), :].T
 
-    def near_block(chip, late=None):
+    def near_block(chip, last=False):
         result = lax.dot_general(
             lhs[...].reshape(5 * nep, m), xbuf[place(0, c, chip, 0, hp), :], LAST, preferred_element_type=F32
         )
         rotated = rot[:, pl.ds(pl.multiple_of(chip * hp, hp), hp)].astype(F32)
         each = [jnp.sum(rotated * result[w * nep : w * nep + ne], axis=0, keepdims=True) for w in range(4)]
-        density = jnp.concatenate(each, axis=0).astype(BF16)
-        if late is None:
+        if last:
+            dlast[0, me] = jnp.concatenate(each[:2], axis=0).astype(BF16)
+            dguest[...] = jnp.concatenate(each[2:], axis=0).astype(BF16)
+        else:
+            density = jnp.concatenate(each, axis=0).astype(BF16)
             dbuf[c, q, :, pl.ds(pl.multiple_of(chip * hp, hp), hp)] = density
-        else:
-            dlate[me, :, late * hp : (late + 1) * hp] = density
         s1[:, columns(0, c, chip)] = result[4 * nep : 5 * nep]
 
     def block(second, core, chip):
@@ -183,9 +203,9 @@
     def ways(step):
         return range(2 if step < final else 1)
 
-    def near_blocks(step, late=None):
+    def near_blocks(step):
         for way in ways(step):
-            near_block(from_chip(way, step), None if late is None else late + way)
+            near_block(from_chip(way, step), step == final)
 
     def far_blocks(second, step):
         for way in ways(step):
@@ -207,25 +227,21 @@
         flips = [bit for bit in range(k.bit_length()) if k >> bit & 1]
         return me + sum((1 - 2 * (me // 2**bit % 2)) * 2**bit for bit in flips)
 
-    spans = (pl.ds(0, 2 * hp), pl.ds(2 * hp, hp))
-
-    def send_late(group):
-        for k in order:
-            start(remote(dlate.at[me, :, spans[group]], late_recv.at[group], peer(k)))
-
-    def spread_rows(value, chip, where):
-        for part in range(2):
-            dfull[part * n + 2 * chip : part * n + 2 * chip + 2, where] = value[2 * part : 2 * part + 2].astype(F32)
-
-    def gather_late(group):
-        arrived(dlate.at[pl.ds(0, n - 1), :, spans[group]], late_recv.at[group])
-        for s in range(n):
-            chip = s // 2
-            pos = chip // 2 if chip % 2 == 0 else h - 1 - chip // 2
-            for i in ((0, 1), (2,))[group]:
-                other = chip_at(pos + (1 - final, final - 1, final)[i])
-                first = (s % 2) * run + other * hp
-                spread_rows(dlate[s, :, i * hp : (i + 1) * hp], chip, slice(first, first + hp))
+    def send_last():
+        for k in range(n - 1, -1, -1):
+            target = peer(k)
+            if k:
+                start(remote(dlast.at[0, me], last_recv.at[0], target))
+            start(remote(dguest, last_recv.at[1], {"parts": 1 - here, "chol": target}, dlast.at[1, me]))
+
+    def gather_last():
+        for guest in range(2):
+            arrived(dlast.at[guest, pl.ds(0, n - 1 + guest)], last_recv.at[guest])
+            for s in range(n):
+                chip = s // 2
+                pos = chip // 2 if chip % 2 == 0 else h - 1 - chip // 2
+                first = guest * side + (s % 2) * run + chip_at(pos + final) * hp
+                dtail[2 * chip : 2 * chip + 2, first : first + hp] = dlast[guest, s].astype(F32)
 
     block(1, c, q)
     arrived(xbuf.at[pl.ds(0, p)], mine_recv)
@@ -242,53 +258,59 @@
     for step in range(2, final):
         take_both(step, 0, 1)
         near_blocks(step - 1)
-        if step == final - 1:
-            for k in range(1, h):
-                start(remote(dbuf.at[c, q], dens_recv, (q + k) % h * 2 + c))
         take_both(step, 2)
         if step < final - 1:
             far_blocks(0, step - 1)
             turns(step - 1)
         take_both(step, 3)
+    near_blocks(final - 1)
+    for k in range(1, h):
+        start(remote(dbuf.at[c, q], dens_recv, (q + k) % h * 2 + c))
     for kind in (4, 5):
         for way in range(2):
             start(hop(way, 1, kind))
-    near_blocks(final - 1, 0)
     pl.semaphore_wait(ready_sem, 1)
-    send_late(0)
+    signal(all_sem, {"parts": 1 - here})
     for way in range(2):
         across(way, 1)
     far_blocks(0, final - 2)
     turns(final - 2)
     take_both(final, 0, 1, 2, 3)
-    near_blocks(final, 2)
-    send_late(1)
+    near_blocks(final)
+    pl.semaphore_wait(all_sem, 1)
+    send_last()
+    for kind in (0, 1):
+        share(0, final, kind)
     for way in range(2):
         across(way, 2)
     take_both(1, 4)
+    arrived(dbuf.at[c, pl.ds(0, h - 1)], dens_recv)
+    start(remote(dbuf.at[c], dpair_recv, partner))
     far_blocks(0, final - 1)
     turns(final - 1)
     take_both(1, 5)
-    arrived(dbuf.at[c, pl.ds(0, h - 1)], dens_recv)
-    start(remote(dbuf.at[c], dpair_recv, partner))
     fields_copy.wait()
     pltpu.make_async_copy(core_ref, corep, core_sem).wait()
-    second_blocks(1)
     arrived(dbuf.at[1 - c], dpair_recv)
     for s in range(n):
-        spread_rows(dbuf[s % 2, s // 2], s // 2, slice((s % 2) * run, (s % 2 + 1) * run))
-    gather_late(0)
-    take_both(2, 4)
-    gather_late(1)
+        for part in range(2):
+            rows = slice(part * n + 2 * (s // 2), part * n + 2 * (s // 2) + 2)
+            value = dbuf[s % 2, s // 2, 2 * part : 2 * part + 2]
+            dfull[rows, (s % 2) * run : (s % 2 + 1) * run] = value.astype(F32)
     partial = lax.dot_general(dfull[...].astype(BF16), corep[:, 0:side], LAST, preferred_element_type=F32)
     fpart[...] = partial[n : 2 * n]
     start(remote(fpart, swap_recv, {"parts": 1 - here}, fother))
+    for kind in (2, 3):
+        share(0, final, kind)
+    for way in range(2):
+        share(way, final - 1, 3)
+    second_blocks(1)
+    take_both(2, 4)
+    gather_last()
+    last = lax.dot_general(dtail[...].astype(BF16), corep[...], LAST, preferred_element_type=F32)
     take_both(2, 5)
-    for step in range(3, final):
-        for way in range(2):
-            across(way, step)
     arrived(fother, swap_recv)
-    force_bias = partial[0:n] + fother[...]
+    force_bias = partial[0:n] + fother[...] + last
     fb_ref[...] = force_bias
     shifted = (fields[...] - force_bias).astype(BF16)
     potentials = []
@@ -304,15 +326,18 @@
             copy = remote(pbuf.at[a, target], pot_recv.at[a], target, rbuf.at[a, k - 1], pot_send)
             copy.start()
             potentials.append(copy)
-    take_both(3, 4)
+    for way in range(2):
+        across(way, final - 1)
     second_blocks(2)
-    take_both(3, 5)
     far_blocks(0, final)
     turns(final)
-    across(0, final)
-    take_both(final, 4, 5)
-    second_blocks(3)
+    for way in range(2):
+        across(way, final)
+    take_both(final - 1, 4)
+    for way in range(2):
+        across_extra(way)
     second_blocks(final)
+    second_blocks(final - 1)
     for copy in sent:
         copy.wait_send()
 
@@ -385,8 +410,10 @@
             pltpu.VMEM((nep, points), F32),
             pltpu.VMEM((nep, points), BF16),
             pltpu.VMEM((2, h, 4, run), BF16),
-            pltpu.VMEM((n, 4, 3 * hp), BF16),
+            pltpu.VMEM((2, n, 2, hp), BF16),
+            pltpu.VMEM((2, hp), BF16),
             pltpu.VMEM((2 * n, side), F32),
+            pltpu.VMEM((n, points), F32),
             pltpu.VMEM(fields.shape, F32),
             pltpu.VMEM(fields.shape, F32),
             pltpu.VMEM((2, n, 2, run), BF16),
@@ -397,8 +424,10 @@
             pltpu.VMEM((nep, m), F32),
             *[dma(())] * 15,
             pltpu.SemaphoreType.REGULAR,
+            pltpu.SemaphoreType.REGULAR,
             dma((2, h // 2, 6)),
             dma((2, h // 2)),
+            dma((2,)),
             dma((2, 2, h // 2)),
             dma((2,)),
             dma((2,)),

time: 54.2 us -> 51.6 us (0.952)
  Pallas kernels: 53.3 us -> 50.6 us
    pallas_call x1, Pallas kernels: 52.5 us -> 49.8 us  [fused(): pl.pallas_call(functools.partial(kernel, n), out_shape=(pltpu.VMEM((ne, m...]
where the time goes in v4:
time: 51.6 us; the launch traced here: 51.4 us
  Pallas kernels  50.6 us (98%)
  between operations  0.8 us (2%)
    pallas_call x1, Pallas kernels, fused(): pl.pallas_call(functools.partial(kernel, n), out_shape=(pltpu.VMEM((ne, m...  49.8 us

profile of v4, /device:TPU:0, one launch (start us, length us, event | category | flops | bytes accessed | tf_op | source)
XLA Modules:
  0.0 51.4 jit_solution(926019438401896192)
XLA Ops:
  0.6 49.8 %shard_map.77 = (f32[100,8,128]{2,1,0:T(8,128)S(1)}, f32[16,64]{1,0:T(8,128)S(1)}) custom-call(f32[100,8,128]{2,1,0:T(8,128)} %bitcast.3, f32[100,1,100]{2,1,0:T(1,128)} %bitcast.4, bf16[256,1024]{1,0:T(8,128)(2,1)} %rows_ref.1, bf16[100,4096]{1,0:T(8,128)(2,1)} %rot_ref.1, bf16[64,4096]{1,0:T(8,128)(2,1)} %core_ref.1, f32[16,64]{1,0:T(8,128)} %fields_ref.1), custom_call_target="tpu_custom_call" | custom-call | tf_op jit(solution)/shard_map/pallas_call | solution.py:395
  50.5 0.8 %shard_map.78 = (f32[100,8,128]{2,1,0:T(8,128)}, f32[16,64]{1,0:T(8,128)}) custom-call(f32[100,8,128]{2,1,0:T(8,128)S(1)} %get-tuple-element.6.propagated, f32[16,64]{1,0:T(8,128)S(1)} %get-tuple-element.7.force_bias), custom_call_target="tpu_custom_call" | custom-call | tf_op jit(solution)/shard_map/pallas_call | solution.py:444

commit v5 on v4

--- a/solution.py
+++ b/solution.py
@@ -143,6 +143,19 @@
             start(hop(way, 1, kind))
     for second in range(2):
         start(remote(xbuf.at[place(second, c, q, 0, hp)], mine_recv, partner))
+    for near in ring:
+        signal(hello_sem.at[0], near)
+
+    total[ne:nep] = jnp.zeros((nep - ne, m), F32)
+    pad[ne:nep] = jnp.zeros((nep - ne, m), F32)
+    orb_copy.wait()
+    for j in range(m // 128):
+        total[0:ne, j * 128 : (j + 1) * 128] = orb3[:, j]
+    inv_copy.wait()
+    pad[0:ne] = jnp.dot(inv[:, 0], total[0:ne], preferred_element_type=F32, precision=lax.Precision.HIGHEST)
+    lhs[c] = pad[...].astype(BF16)
+    start(remote(lhs.at[c], guest_recv, {"parts": 1 - here}, lhs.at[2 + c]))
+    start(remote(lhs.at[c], pair_recv, partner))
     for chip in range(h):
         first = pl.multiple_of((chip * 2 + c) * p + here * hp, hp)
         pltpu.make_async_copy(rot_ref.at[:, pl.ds(first, hp)], rot.at[:, pl.ds(chip * hp, hp)], rot_sem).start()
@@ -154,20 +167,7 @@
                 corep.at[:, pl.ds(second * side + (s % 2) * run + (s // 2) * hp, hp)],
                 core_sem,
             ).start()
-    for near in ring:
-        signal(hello_sem.at[0], near)
-
-    pad[...] = jnp.zeros_like(pad)
-    orb_copy.wait()
-    for j in range(m // 128):
-        pad[0:ne, j * 128 : (j + 1) * 128] = orb3[:, j]
-    total[...] = pad[...]
-    lhs[4] = pad[...].astype(BF16)
-    inv_copy.wait()
-    pad[0:ne] = jnp.dot(inv[:, 0], pad[0:ne], preferred_element_type=F32, precision=lax.Precision.HIGHEST)
-    lhs[c] = pad[...].astype(BF16)
-    start(remote(lhs.at[c], guest_recv, {"parts": 1 - here}, lhs.at[2 + c]))
-    start(remote(lhs.at[c], pair_recv, partner))
+    lhs[4] = total[...].astype(BF16)
     dbuf[c, q] = jnp.zeros(dbuf.shape[2:], BF16)
     dtail[...] = jnp.zeros_like(dtail)
     for k in range(1, h // 2 - 1):
@@ -175,7 +175,6 @@
         for near in ring:
             signal(hello_sem.at[k], near)
     arrived(lhs.at[1 - c], pair_recv)
-    pltpu.make_async_copy(rot_ref.at[:, pl.ds(0, run)], rot, rot_sem).wait()
 
     def turn(second, core, chip):
         xturn[:, columns(second, core, chip)] = xbuf[place(second, core, chip, 0, hp), :].T
@@ -253,6 +252,7 @@
     arrived(lhs.at[2 + c], guest_recv)
     start(remote(lhs.at[2 + c], share_recv, partner))
     arrived(lhs.at[3 - c], share_recv)
+    pltpu.make_async_copy(rot_ref.at[:, pl.ds(0, run)], rot, rot_sem).wait()
     near_block(q)
     turn(0, c, q)
     for step in range(2, final):
@@ -264,8 +264,8 @@
             turns(step - 1)
         take_both(step, 3)
     near_blocks(final - 1)
-    for k in range(1, h):
-        start(remote(dbuf.at[c, q], dens_recv, (q + k) % h * 2 + c))
+    for k in range(h - 1, 0, -1):
+        start(remote(dbuf.at[c, q], dens_recv, peer(2 * k)))
     for kind in (4, 5):
         for way in range(2):
             start(hop(way, 1, kind))
@@ -275,11 +275,13 @@
         across(way, 1)
     far_blocks(0, final - 2)
     turns(final - 2)
-    take_both(final, 0, 1, 2, 3)
+    take_both(final, 0)
+    share(0, final, 0)
+    take_both(final, 1, 2, 3)
     near_blocks(final)
     pl.semaphore_wait(all_sem, 1)
     send_last()
-    for kind in (0, 1):
+    for kind in (1, 2):
         share(0, final, kind)
     for way in range(2):
         across(way, 2)
@@ -300,15 +302,13 @@
     partial = lax.dot_general(dfull[...].astype(BF16), corep[:, 0:side], LAST, preferred_element_type=F32)
     fpart[...] = partial[n : 2 * n]
     start(remote(fpart, swap_recv, {"parts": 1 - here}, fother))
-    for kind in (2, 3):
-        share(0, final, kind)
+    share(0, final, 3)
     for way in range(2):
         share(way, final - 1, 3)
     second_blocks(1)
     take_both(2, 4)
     gather_last()
     last = lax.dot_general(dtail[...].astype(BF16), corep[...], LAST, preferred_element_type=F32)
-    take_both(2, 5)
     arrived(fother, swap_recv)
     force_bias = partial[0:n] + fother[...] + last
     fb_ref[...] = force_bias
@@ -326,6 +326,7 @@
             copy = remote(pbuf.at[a, target], pot_recv.at[a], target, rbuf.at[a, k - 1], pot_send)
             copy.start()
             potentials.append(copy)
+    take_both(2, 5)
     for way in range(2):
         across(way, final - 1)
     second_blocks(2)
@@ -334,9 +335,9 @@
     for way in range(2):
         across(way, final)
     take_both(final - 1, 4)
+    second_blocks(final)
     for way in range(2):
         across_extra(way)
-    second_blocks(final)
     second_blocks(final - 1)
     for copy in sent:
         copy.wait_send()
@@ -348,9 +349,9 @@
         arrived(rbuf.at[a], pot_recv.at[a])
         for k in order:
             summed = summed + rbuf[a, k - 1].astype(F32)
-        pot[a] = summed
         for core in range(2):
             where = slice(a * side + core * run, a * side + (core + 1) * run)
+            pot[:, where] = summed[core : core + 1]
             sc[:, where] = (s1[:, where] * summed[core : core + 1]).astype(BF16)
         for j in range(m // wide):
             where = slice(j * wide, (j + 1) * wide)
@@ -362,12 +363,10 @@
                 total[:, where] += result
                 tbf[:, where] = result.astype(BF16)
     for order in range(2, TAYLOR + 1):
-        for j in range(n):
-            where = slice(j * p, (j + 1) * p)
-            result = jnp.dot(tbf[...], xturn[:, where], preferred_element_type=F32)
-            a, core, first = j // h, j % h * 2 // h, j % (h // 2) * p
-            scale = pot[a, core : core + 1, first : first + p] / order
-            sc[:, where] = (result * scale).astype(BF16)
+        for a in range(2):
+            half = slice(a * side, (a + 1) * side)
+            result = jnp.dot(tbf[...], xturn[:, half], preferred_element_type=F32)
+            sc[:, half] = (result * (pot[:, half] / order)).astype(BF16)
         for j in range(m // wide):
             where = slice(j * wide, (j + 1) * wide)
             result = jnp.dot(sc[...], xbuf[:, where], preferred_element_type=F32)
@@ -418,7 +417,7 @@
             pltpu.VMEM(fields.shape, F32),
             pltpu.VMEM((2, n, 2, run), BF16),
             pltpu.VMEM((2, n - 1, 2, run), BF16),
-            pltpu.VMEM((2, 2, run), F32),
+            pltpu.VMEM((1, points), F32),
             pltpu.VMEM((nep, m), BF16),
             pltpu.VMEM((nep, m), F32),
             pltpu.VMEM((nep, m), F32),

time: 51.6 us -> 51.1 us (level)
  Pallas kernels: 50.6 us -> 49.8 us
    pallas_call x1, Pallas kernels: 49.8 us -> 49 us  [fused(): pl.pallas_call(functools.partial(kernel, n), out_shape=(pltpu.VMEM((ne, m...]
where the time goes in v5:
time: 51.1 us; the launch traced here: 50.6 us
  Pallas kernels  49.8 us (97%)
  between operations  0.8 us (2%)
    pallas_call x1, Pallas kernels, fused(): pl.pallas_call(functools.partial(kernel, n), out_shape=(pltpu.VMEM((ne, m...  49 us

profile of v5, /device:TPU:0, one launch (start us, length us, event | category | flops | bytes accessed | tf_op | source)
XLA Modules:
  0.0 50.6 jit_solution(11928582646687844212)
XLA Ops:
  0.6 49.0 %shard_map.77 = (f32[100,8,128]{2,1,0:T(8,128)S(1)}, f32[16,64]{1,0:T(8,128)S(1)}) custom-call(f32[100,8,128]{2,1,0:T(8,128)} %bitcast.3, f32[100,1,100]{2,1,0:T(1,128)} %bitcast.4, bf16[256,1024]{1,0:T(8,128)(2,1)} %rows_ref.1, bf16[100,4096]{1,0:T(8,128)(2,1)} %rot_ref.1, bf16[64,4096]{1,0:T(8,128)(2,1)} %core_ref.1, f32[16,64]{1,0:T(8,128)} %fields_ref.1), custom_call_target="tpu_custom_call" | custom-call | tf_op jit(solution)/shard_map/pallas_call | solution.py:394
  49.7 0.8 %shard_map.78 = (f32[100,8,128]{2,1,0:T(8,128)}, f32[16,64]{1,0:T(8,128)}) custom-call(f32[100,8,128]{2,1,0:T(8,128)S(1)} %get-tuple-element.6.propagated, f32[16,64]{1,0:T(8,128)S(1)} %get-tuple-element.7.force_bias), custom_call_target="tpu_custom_call" | custom-call | tf_op jit(solution)/shard_map/pallas_call | solution.py:443

commit v6 on v5

--- a/solution.py
+++ b/solution.py
@@ -180,8 +180,9 @@
         xturn[:, columns(second, core, chip)] = xbuf[place(second, core, chip, 0, hp), :].T
 
     def near_block(chip, last=False):
+        count = 4 if last else 5
         result = lax.dot_general(
-            lhs[...].reshape(5 * nep, m), xbuf[place(0, c, chip, 0, hp), :], LAST, preferred_element_type=F32
+            lhs[0:count].reshape(count * nep, m), xbuf[place(0, c, chip, 0, hp), :], LAST, preferred_element_type=F32
         )
         rotated = rot[:, pl.ds(pl.multiple_of(chip * hp, hp), hp)].astype(F32)
         each = [jnp.sum(rotated * result[w * nep : w * nep + ne], axis=0, keepdims=True) for w in range(4)]
@@ -191,7 +192,8 @@
         else:
             density = jnp.concatenate(each, axis=0).astype(BF16)
             dbuf[c, q, :, pl.ds(pl.multiple_of(chip * hp, hp), hp)] = density
-        s1[:, columns(0, c, chip)] = result[4 * nep : 5 * nep]
+        if not last:
+            s1[:, columns(0, c, chip)] = result[4 * nep : 5 * nep]
 
     def block(second, core, chip):
         s1[:, columns(second, core, chip)] = lax.dot_general(
@@ -331,7 +333,7 @@
         across(way, final - 1)
     second_blocks(2)
     far_blocks(0, final)
-    turns(final)
+    block(0, c, from_chip(0, final))
     for way in range(2):
         across(way, final)
     take_both(final - 1, 4)

time: 51.1 us -> 51.2 us (level)
  no operation moved by 1% of the time
where the time goes in v6:
time: 51.2 us; the launch traced here: 50.7 us
  Pallas kernels  49.9 us (97%)
  between operations  0.8 us (2%)
    pallas_call x1, Pallas kernels, fused(): pl.pallas_call(functools.partial(kernel, n), out_shape=(pltpu.VMEM((ne, m...  49.1 us

profile of v6, /device:TPU:0, one launch (start us, length us, event | category | flops | bytes accessed | tf_op | source)
XLA Modules:
  0.0 50.7 jit_solution(3337772682296096293)
XLA Ops:
  0.6 49.1 %shard_map.77 = (f32[100,8,128]{2,1,0:T(8,128)S(1)}, f32[16,64]{1,0:T(8,128)S(1)}) custom-call(f32[100,8,128]{2,1,0:T(8,128)} %bitcast.3, f32[100,1,100]{2,1,0:T(1,128)} %bitcast.4, bf16[256,1024]{1,0:T(8,128)(2,1)} %rows_ref.1, bf16[100,4096]{1,0:T(8,128)(2,1)} %rot_ref.1, bf16[64,4096]{1,0:T(8,128)(2,1)} %core_ref.1, f32[16,64]{1,0:T(8,128)} %fields_ref.1), custom_call_target="tpu_custom_call" | custom-call | tf_op jit(solution)/shard_map/pallas_call | solution.py:396
  49.8 0.8 %shard_map.78 = (f32[100,8,128]{2,1,0:T(8,128)}, f32[16,64]{1,0:T(8,128)}) custom-call(f32[100,8,128]{2,1,0:T(8,128)S(1)} %get-tuple-element.6.propagated, f32[16,64]{1,0:T(8,128)S(1)} %get-tuple-element.7.force_bias), custom_call_target="tpu_custom_call" | custom-call | tf_op jit(solution)/shard_map/pallas_call | solution.py:445
